TPU v7x, 256 devices: a whole 4x4x8 slice. The times are simulated.
256 devices in a mesh: ctx: 64 (over x, z, core), tp: 4 (over y).
Axes of the slice: x: 4, y: 4, z: 8, core: 2. Of those that a mesh axis runs over, the one named last changes fastest.
Arguments:
- out_gate: bfloat16 [8192, 8192], P('ctx', 'tp'), may hold values from -128 to 128
- key_proj: bfloat16 [8192, 8192], P('ctx', 'tp'), may hold values from -6 to 6
- value_proj: bfloat16 [8192, 8192], P('ctx', 'tp'), may hold values from -6 to 6
- residue: float32 [512, 16], P('tp'), may hold values from -1 to 1
- log_decay: float32 [512, 16], P('tp'), may hold values from -13 to -3
- skip: float32 [8192], P('tp'), may hold values from -4 to 4
- gain: float32 [8192], P('tp'), may hold values from 0.1 to 1.9
- cotangent: bfloat16 [8192, 8192], P('ctx', 'tp'), may hold values from -6 to 6
Outputs:
- mixer_out: bfloat16 [8192, 8192], P('ctx', 'tp')
- grad_q: bfloat16 [8192, 8192], P('ctx', 'tp')
- grad_k: bfloat16 [8192, 8192], P('ctx', 'tp')
- grad_v: bfloat16 [8192, 8192], P('ctx', 'tp')
- grad_residue: float32 [512, 16], P('tp')
- grad_log_decay: float32 [512, 16], P('tp')
All inputs are finite; a program needn't handle non-finite values.
Results may differ from a plain program's by a relative error of at most 0.0013.
Values sent between devices are 32-bit elements; how exact they have to be, the bound alone decides.
No kernel may reach another device: no remote copies, remote signals or barrier semaphores. Data moves between devices by JAX's collectives and lax.ppermute only.
A program may use at most 128 MiB of HBM per device.

v0:
```python
import jax
import jax.numpy as jnp
from jax import lax
from jax.sharding import PartitionSpec as P

EPSILON = 1e-06
HIGHEST_ACCURACY = lax.Precision.HIGHEST


def prefix(value, axis, combine, identity, reverse):
    count, here = (lax.axis_size(axis), lax.axis_index(axis))
    everything = jax.tree.map(lambda part: lax.all_gather(part, axis), value)
    start = jax.tree.map(
        lambda part, zero: jnp.broadcast_to(jnp.asarray(zero, part.dtype), part.shape),
        value,
        identity,
    )

    def step(k, before):
        at = count - 1 - k if reverse else k
        reached = at > here if reverse else at < here
        new = combine(before, jax.tree.map(lambda part: part[at], everything))
        return jax.tree.map(lambda a, b: jnp.where(reached, a, b), new, before)

    return lax.fori_loop(0, count, step, start)


def toeplitz_block(taps_ext, first_row, row_count, span):
    row_ids = first_row + jnp.arange(row_count, dtype=jnp.int32)

    def toeplitz_one_row(row_id):
        return lax.dynamic_slice_in_dim(taps_ext, span - 1 - row_id, span, 0)

    return jax.vmap(toeplitz_one_row)(row_ids)


def shear_rows(product, first_row, span):
    row_count = product.shape[0]
    extended = jnp.concatenate([jnp.flip(product, 1), jnp.zeros_like(product)], axis=1)
    row_ids = first_row + jnp.arange(row_count, dtype=jnp.int32)

    def shear_one_row(row_data, row_id):
        return lax.dynamic_slice_in_dim(row_data, span - 1 - row_id, span, 0)

    return jnp.sum(jax.vmap(shear_one_row)(extended, row_ids), axis=0)


def join_forward(earlier, later_part):
    state_early, moment_early, decay_early, length_early = earlier
    state_late, moment_late, decay_late, length_late = later_part
    factor = decay_late[:, None, :]
    state_new = factor * state_early + state_late
    moment_new = factor * (moment_early + length_late[0] * state_early) + moment_late
    return (state_new, moment_new, decay_early * decay_late, length_early + length_late)


def join_backward(earlier, later_part):
    state_early, decay_early = earlier
    state_late, decay_late = later_part
    return (decay_late[:, None, :] * state_early + state_late, decay_early * decay_late)


def per_device(out_gate, key_proj, value_proj, residue, log_decay, skip, gain, cotangent):
    block_len, channel_count = out_gate.shape
    groups, modes = residue.shape
    members = channel_count // groups
    shard_total = lax.axis_size("ctx")
    token_total = block_len * shard_total
    full_width = channel_count * lax.axis_size("tp")
    sub_len = min(block_len, 128)
    sub_count = block_len // sub_len
    row_block = min(sub_len, 32)
    gate_full = out_gate.astype(jnp.float32)
    key_full = key_proj.astype(jnp.float32)
    value_full = value_proj.astype(jnp.float32)
    signal = key_full * value_full
    grid_signal = signal.reshape(block_len, groups, members).transpose(0, 2, 1)
    rate_table = jnp.exp(log_decay).T
    residue_table = residue.T
    lag_index = jnp.arange(block_len, dtype=jnp.float32)
    head_decay = jnp.exp(-rate_table[:, None, :] * lag_index[None, :, None])
    back_head = jnp.flip(head_decay, 1)
    own_state = jnp.einsum("rsg,scg->rcg", back_head, grid_signal, precision=HIGHEST_ACCURACY)
    own_moment = jnp.einsum(
        "rsg,scg->rcg",
        back_head * jnp.flip(lag_index)[None, :, None],
        grid_signal,
        precision=HIGHEST_ACCURACY,
    )
    step_decay = jnp.exp(-rate_table * block_len)
    zero_state = jnp.zeros_like(own_state)
    own_length = jnp.full((1,), block_len, jnp.float32)
    identity = (zero_state, zero_state, jnp.ones_like(step_decay), jnp.zeros((1,), jnp.float32))
    state_in, moment_in, _, _ = prefix(
        (own_state, own_moment, step_decay, own_length), "ctx", join_forward, identity, False
    )
    sub_signal = grid_signal.reshape(sub_count, sub_len, members, groups)
    sub_index = jnp.arange(sub_len, dtype=jnp.float32)
    segment_head = jnp.exp(-rate_table[:, None, :] * sub_index[None, :, None])
    segment_trail = jnp.exp(-rate_table[:, None, :] * (sub_index + 1.0)[None, :, None])
    sub_back = jnp.flip(segment_head, 1)
    segment_taps = jnp.sum(residue_table[:, None, :] * segment_head, axis=0)
    taps_ext = jnp.concatenate([jnp.flip(segment_taps, 0), jnp.zeros_like(segment_taps)], axis=0)
    block_number = jnp.arange(sub_count, dtype=jnp.float32)
    later_number = block_number[:, None]
    earlier_number = block_number[None, :]
    gap_before = jnp.maximum(later_number - 1.0 - earlier_number, 0.0) * sub_len
    mask_before = (earlier_number < later_number).astype(jnp.float32)
    pass_before = (
        jnp.exp(-rate_table[:, None, None, :] * gap_before[None, :, :, None])
        * mask_before[None, :, :, None]
    )
    start_offset = sub_len * block_number
    start_decay = jnp.exp(-rate_table[:, None, :] * start_offset[None, :, None])
    sub_state = jnp.einsum("rsg,nscg->nrcg", sub_back, sub_signal, precision=HIGHEST_ACCURACY)
    sub_moment = jnp.einsum(
        "rsg,nscg->nrcg",
        sub_back * jnp.flip(sub_index)[None, :, None],
        sub_signal,
        precision=HIGHEST_ACCURACY,
    )
    incoming_state = jnp.einsum(
        "rnig,ircg->nrcg", pass_before, sub_state, precision=HIGHEST_ACCURACY
    )
    incoming_state = incoming_state + jnp.einsum(
        "rng,rcg->nrcg", start_decay, state_in, precision=HIGHEST_ACCURACY
    )
    enter_moment = jnp.einsum(
        "rnig,ircg->nrcg", pass_before, sub_moment, precision=HIGHEST_ACCURACY
    )
    enter_moment = enter_moment + jnp.einsum(
        "rnig,ircg->nrcg",
        pass_before * gap_before[None, :, :, None],
        sub_state,
        precision=HIGHEST_ACCURACY,
    )
    enter_moment = enter_moment + jnp.einsum(
        "rng,rcg->nrcg", start_decay, moment_in, precision=HIGHEST_ACCURACY
    )
    enter_moment = enter_moment + jnp.einsum(
        "rng,rcg->nrcg",
        start_decay * start_offset[None, :, None],
        state_in,
        precision=HIGHEST_ACCURACY,
    )
    carried = jnp.einsum(
        "rug,nrcg->nucg",
        residue_table[:, None, :] * segment_trail,
        incoming_state,
        precision=HIGHEST_ACCURACY,
    )
    matrices = []
    local_parts = []
    for row_start in range(0, sub_len, row_block):
        matrix = toeplitz_block(taps_ext, row_start, row_block, sub_len)
        matrices.append(matrix)
        local_parts.append(
            jnp.einsum("tsg,nscg->ntcg", matrix, sub_signal, precision=HIGHEST_ACCURACY)
        )
    local_grid = jnp.concatenate(local_parts, axis=1) + carried
    convolved = (
        local_grid.reshape(block_len, members, groups)
        .transpose(0, 2, 1)
        .reshape(block_len, channel_count)
    )
    mixed = convolved + skip * signal
    premix = gate_full * mixed
    squares = lax.psum(jnp.sum(premix * premix, axis=1), "tp")
    inverse = lax.rsqrt(squares / full_width + EPSILON)[:, None]
    normed = premix * inverse
    mixer_out = (normed * gain).astype(jnp.bfloat16)
    pull = cotangent.astype(jnp.float32) * gain
    inner = lax.psum(jnp.sum(pull * normed, axis=1), "tp")
    dpre = (pull - normed * (inner / full_width)[:, None]) * inverse
    grad_q = (dpre * mixed).astype(jnp.bfloat16)
    weight = dpre * gate_full
    grid_weight = weight.reshape(block_len, groups, members).transpose(0, 2, 1)
    local_leading_part = jnp.einsum(
        "rsg,scg->rcg", head_decay, grid_weight, precision=HIGHEST_ACCURACY
    )
    after_state, _ = prefix(
        (local_leading_part, step_decay),
        "ctx",
        join_backward,
        (zero_state, jnp.ones_like(step_decay)),
        True,
    )
    segment_weight = grid_weight.reshape(sub_count, sub_len, members, groups)
    gap_after = jnp.maximum(earlier_number - later_number - 1.0, 0.0) * sub_len
    mask_after = (earlier_number > later_number).astype(jnp.float32)
    pass_after = (
        jnp.exp(-rate_table[:, None, None, :] * gap_after[None, :, :, None])
        * mask_after[None, :, :, None]
    )
    end_decay = jnp.exp(
        -rate_table[:, None, :] * (sub_len * (sub_count - 1.0 - block_number))[None, :, None]
    )
    segment_leading = jnp.einsum(
        "rug,nucg->nrcg", segment_head, segment_weight, precision=HIGHEST_ACCURACY
    )
    after_sub = jnp.einsum(
        "rnig,ircg->nrcg", pass_after, segment_leading, precision=HIGHEST_ACCURACY
    )
    after_sub = after_sub + jnp.einsum(
        "rng,rcg->nrcg", end_decay, after_state, precision=HIGHEST_ACCURACY
    )
    back_cross = jnp.einsum(
        "rsg,nrcg->nscg",
        residue_table[:, None, :] * jnp.flip(segment_trail, 1),
        after_sub,
        precision=HIGHEST_ACCURACY,
    )
    back_local = jnp.zeros_like(segment_weight)
    lagged = jnp.zeros((sub_len, groups), jnp.float32)
    for block_id, row_start in enumerate(range(0, sub_len, row_block)):
        band_weight = segment_weight[:, row_start : row_start + row_block]
        back_local = back_local + jnp.einsum(
            "tsg,ntcg->nscg", matrices[block_id], band_weight, precision=HIGHEST_ACCURACY
        )
        product = jnp.einsum("ntcg,nscg->tsg", band_weight, sub_signal, precision=HIGHEST_ACCURACY)
        lagged = lagged + shear_rows(product, row_start, sub_len)
    back_grid = back_local + back_cross
    grad_signal = (
        back_grid.reshape(block_len, members, groups)
        .transpose(0, 2, 1)
        .reshape(block_len, channel_count)
        + skip * weight
    )
    grad_k = (grad_signal * value_full).astype(jnp.bfloat16)
    grad_v = (grad_signal * key_full).astype(jnp.bfloat16)
    pair_sums = jnp.einsum(
        "ntcg,nrcg->rntg", segment_weight, incoming_state, precision=HIGHEST_ACCURACY
    )
    pair_moment = jnp.einsum(
        "ntcg,nrcg->rntg", segment_weight, enter_moment, precision=HIGHEST_ACCURACY
    )
    tail_wide = segment_trail[:, None, :, :]
    residue_part = jnp.sum(tail_wide * pair_sums, axis=(1, 2)) + jnp.sum(
        segment_head * lagged[None], axis=1
    )
    moment_part = jnp.sum(
        tail_wide * ((sub_index + 1.0)[None, None, :, None] * pair_sums + pair_moment), axis=(1, 2)
    )
    moment_part = moment_part + jnp.sum(
        segment_head * sub_index[None, :, None] * lagged[None], axis=1
    )
    residue_total, moment_total = lax.psum((residue_part.T, moment_part.T), "ctx")
    grad_residue = residue_total / token_total
    grad_log_decay = -residue * jnp.exp(log_decay) * moment_total / token_total
    return (mixer_out, grad_q, grad_k, grad_v, grad_residue, grad_log_decay)


def solution(mesh):
    placed = (
        P("ctx", "tp"),
        P("ctx", "tp"),
        P("ctx", "tp"),
        P("tp", None),
        P("tp", None),
        P("tp"),
        P("tp"),
        P("ctx", "tp"),
    )
    return jax.shard_map(
        per_device,
        mesh=mesh,
        in_specs=placed,
        out_specs=(
            P("ctx", "tp"),
            P("ctx", "tp"),
            P("ctx", "tp"),
            P("ctx", "tp"),
            P("tp", None),
            P("tp", None),
        ),
        check_vma=False,
    )
```

profile of v0, /device:TPU:1, one launch (start us, length us, event | category | flops | bytes accessed | tf_op | source)
XLA Modules:
  0.0 1473.1 jit_solution(11136434318298398852)
XLA Ops:
  21.6 138.0 %while.39 = (s32[]{:T(128)}, f32[256,128]{1,0:T(8,128)S(1)}, s32[32,2]{0,1:T(2,128)S(1)}, f32[32,128,128]{1,0,2:T(8,128)}, s32[]{:T(128)}, /*index=5*/s32[]{:T(128)}) while((s32[]{:T(128)}, f32[256,128]{1,0:T(8,128)S(1)}, s32[32,2]{0,1:T(2,128)S(1)}, f32[32,128,128]{1,0,2:T(8,128)}, s32[]{:T(128)}, /*index=5*/s32[]{:T(128)}) %tuple.158), condition=%wide.while_cond.3, body=%wide.while_body.3.sunk | while | flops 2 | bytes 393329 | solution.py:32
  161.2 137.5 %while.38 = (s32[]{:T(128)}, f32[256,128]{1,0:T(8,128)S(1)}, s32[32,2]{0,1:T(2,128)S(1)}, f32[32,128,128]{1,0,2:T(8,128)}, s32[]{:T(128)}, /*index=5*/s32[]{:T(128)}) while((s32[]{:T(128)}, f32[256,128]{1,0:T(8,128)S(1)}, s32[32,2]{0,1:T(2,128)S(1)}, f32[32,128,128]{1,0,2:T(8,128)}, s32[]{:T(128)}, /*index=5*/s32[]{:T(128)}) %tuple.179), condition=%wide.while_cond.2, body=%wide.while_body.2.sunk | while | flops 2 | bytes 393329 | solution.py:32
  305.2 128.0 %all-reduce.9 = f32[64]{0:T(128)S(1)} all-reduce(f32[64]{0:T(128)S(1)} %dynamic-update-slice.8), channel_id=1, replica_groups=mesh['ctx'=64,'tp'=4] {'ctx'}, use_global_device_ids=true, to_apply=%add.9 | all-reduce | flops 64 | bytes 512
  433.3 52.5 %all-gather = f32[1024,128]{1,0:T(8,128)S(1)} all-gather(f32[16,128]{1,0:T(8,128)S(1)} %get-tuple-element.556), channel_id=2, replica_groups=mesh['ctx'=64,'tp'=4] {'ctx'}, dimensions={0}, use_global_device_ids=true | all-gather | bytes 532480 | tf_op jit(solution)/shard_map/all_gather | solution.py:12
  485.8 6.1 convolution_bitcast_fusion.7
  491.9 4.4 convolution_bitcast_fusion.8
  497.9 142.5 %while.37 = (s32[]{:T(128)}, f32[256,128]{1,0:T(8,128)S(1)}, s32[32,2]{0,1:T(2,128)S(1)}, f32[32,128,128]{1,0,2:T(8,128)}, s32[]{:T(128)}, /*index=5*/s32[]{:T(128)}) while((s32[]{:T(128)}, f32[256,128]{1,0:T(8,128)S(1)}, s32[32,2]{0,1:T(2,128)S(1)}, f32[32,128,128]{1,0,2:T(8,128)}, s32[]{:T(128)}, /*index=5*/s32[]{:T(128)}) %tuple.180), condition=%wide.while_cond.1, body=%wide.while_body.1.sunk | while | flops 2 | bytes 393329 | solution.py:32
  640.4 5.9 convolution_bitcast_fusion.9
  648.0 137.6 %while.36 = (s32[]{:T(128)}, f32[256,128]{1,0:T(8,128)S(1)}, s32[32,2]{0,1:T(2,128)S(1)}, f32[32,128,128]{1,0,2:T(8,128)}, s32[]{:T(128)}, /*index=5*/s32[]{:T(128)}) while((s32[]{:T(128)}, f32[256,128]{1,0:T(8,128)S(1)}, s32[32,2]{0,1:T(2,128)S(1)}, f32[32,128,128]{1,0,2:T(8,128)}, s32[]{:T(128)}, /*index=5*/s32[]{:T(128)}) %tuple.181), condition=%wide.while_cond, body=%wide.while_body.sunk | while | flops 2 | bytes 393329 | solution.py:32
  785.6 5.9 convolution_bitcast_fusion.10
  791.5 149.0 %while.40 = (s32[]{:T(128)}, f32[16,16,128]{2,1,0:T(8,128)S(1)}, f32[16,16,128]{2,1,0:T(8,128)S(1)}, s32[]{:T(128)}, f32[64,16,128]{2,1,0:T(8,128)S(1)}, /*index...) while((s32[]{:T(128)}, f32[16,16,128]{2,1,0:T(8,128)S(1)}, ...), condition=%wide.region_2.3_spmd.clone, body=%wide.region_1.2_spmd.clone.sunk | while | flops 327684 | bytes 811161 | solution.py:25
  941.9 4.9 fusion.3
  947.3 8.8 psum.28
  957.6 6.2 psum.29
  977.9 5.1 convolution_bitcast_fusion
  990.5 5.1 convolution_bitcast_fusion.1
  1003.5 4.9 convolution_bitcast_fusion.3
  1016.0 5.1 convolution_bitcast_fusion.2
  1032.9 6.1 gather_fusion.3
  1045.1 6.1 gather_fusion.2
  1057.2 6.1 gather_fusion
  1069.2 6.1 gather_fusion.1
  1093.0 244.8 %all-reduce.10 = (f32[128,16]{0,1:T(8,128)S(1)}, f32[128,16]{0,1:T(8,128)S(1)}) all-reduce(f32[128,16]{0,1:T(8,128)S(1)} %add_bitcast_fusion.1, f32[128,16]{0,1:T(8,128)S(1)} %add_bitcast_fusion), channel_id=1, replica_groups=mesh['ctx'=64,'tp'=4] {'ctx'}, use_global_device_ids=true, to_apply=%region_15.16 | all-reduce | flops 4096 | bytes 32768 | tf_op jit(solution)/shard_map/psum | solution.py:247
  1349.5 110.1 %while.41 = (s32[]{:T(128)}, f32[16,16,128]{2,1,0:T(8,128)S(1)}, s32[]{:T(128)}, f32[64,16,128]{2,1,0:T(8,128)}, f32[64,16,16,128]{3,2,1,0:T(8,128)}, /*index=5*/s32[]{:T(128)}, s32[]{:T(128)}, s32[]{:T(128)}, s32[]{:T(128)}) while((s32[]{:T(128)}, f32[16,16,128]{2,1,0:T(8,128)S(1)}, s32[]{:T(128)}, f32[64,16,128]{2,1,0:T(8,128)}, ...), condition=%wide.region_8.9_spmd.clone, body=%wide.region_7.8_spmd.clone.sunk | while | flops 131080 | bytes 417967 | solution.py:25
  (1120 shorter events, 941.6 us)
Async XLA Ops:
  7.2 2.9 copy-start.18
  7.2 3.0 copy-start.23
  7.2 784.4 %all-gather.8.cloned.1.call-start = ((), (), s32[]{:S(2)}) async-start(), calls=%async_computation | async-start | bytes 8519680 | tf_op jit(solution)/shard_map/all_gather | solution.py:12
  8.6 2.9 copy-start.6
  14.4 777.1 %all-gather.10.cloned.1.call-start = ((), (), s32[]{:S(2)}) async-start(), calls=%async_computation.1 | async-start | bytes 8519680 | tf_op jit(solution)/shard_map/all_gather | solution.py:12
  19.6 1329.8 %all-gather.12.cloned.1.call-start = ((), (), s32[]{:S(2)}) async-start(), calls=%async_computation.2 | async-start | bytes 8519680 | tf_op jit(solution)/shard_map/all_gather | solution.py:12
  161.1 139.7 %copy-start.13 = (bf16[128,2048]{1,0:T(8,128)(2,1)S(1)}, bf16[128,2048]{1,0:T(8,128)(2,1)}, u32[]{:S(2)}) copy-start(bf16[128,2048]{1,0:T(8,128)(2,1)} %param.12) | copy-start | bytes 1572868
  298.7 5.2 copy-start.26
  433.2 508.6 %copy-start.24 = (f32[128]{0:T(128)}, f32[128]{0:T(128)S(1)}, u32[]{:S(2)}) copy-start(f32[128]{0:T(128)S(1)} %iota_add_fusion) | copy-start | bytes 1540
  433.3 507.3 %copy-start.14 = (f32[16,128]{1,0:T(8,128)}, f32[16,128]{1,0:T(8,128)S(1)}, u32[]{:S(2)}) copy-start(f32[16,128]{1,0:T(8,128)S(1)} %get-tuple-element.554) | copy-start | bytes 24580
  433.3 507.3 %copy-start.16 = (f32[16,128]{1,0:T(8,128)}, f32[16,128]{1,0:T(8,128)S(1)}, u32[]{:S(2)}) copy-start(f32[16,128]{1,0:T(8,128)S(1)} %get-tuple-element.555) | copy-start | bytes 24580
  485.8 6.1 copy-start.1
  941.9 4.9 copy-start.5
  941.9 4.9 copy-start.7
  941.9 4.9 copy-start.10
  941.9 4.9 copy-start.21
  946.8 9.2 copy-start.20
  947.3 16.6 %copy-start.4 = (f32[128,2048]{0,1:T(8,128)}, f32[128,2048]{0,1:T(8,128)S(1)}, u32[]{:S(2)}) copy-start(f32[128,2048]{0,1:T(8,128)S(1)} %get-tuple-element.541) | copy-start | bytes 3145732
  1086.3 251.5 %copy-start.19 = (f32[128,16]{0,1:T(8,128)S(1)}, f32[128,16]{0,1:T(8,128)}, u32[]{:S(2)}) copy-start(f32[128,16]{0,1:T(8,128)} %param.16) | copy-start | bytes 24580
  1339.1 3.8 copy-start.3
  1349.4 110.2 %copy-start.15 = (f32[16,128]{1,0:T(8,128)S(1)}, f32[16,128]{1,0:T(8,128)}, u32[]{:S(2)}) copy-start(f32[16,128]{1,0:T(8,128)} %copy-done.14) | copy-start | bytes 24580
  1349.5 110.2 %copy-start.17 = (f32[16,128]{1,0:T(8,128)S(1)}, f32[16,128]{1,0:T(8,128)}, u32[]{:S(2)}) copy-start(f32[16,128]{1,0:T(8,128)} %copy-done.16) | copy-start | bytes 24580
  1461.0 2.9 copy-start.11
  1461.0 2.9 copy-start.22
  (6 other events, 12.7 us)
Sparse Core Ops, SparseCore 0:
  14.6 87.1 all-gather.7
  105.1 79.7 all-gather.9
  972.2 82.7 all-gather.11
where the time goes:
time: 1500 us; the launch traced here: 1470 us
  local copies, waits for them, and re-layouts  747 us (50%)
  blocking collectives  440 us (29%)
  other arithmetic  193 us (13%)
  matrix products  72.7 us (5%)
    gather x640, local copies, waits for them, and re-layouts  553 us
    psum x1, blocking collectives, per_device(): lax.psum((residue_part.T, moment_part.T), 'ctx')  245 us
    select_n x128, other arithmetic, step(): return jax.tree.map(lambda a, b: jnp.where(reached, a, b), new, before)  174 us
    unnamed x1, blocking collectives  128 us
    all_gather x1, blocking collectives, prefix(): everything = jax.tree.map(lambda part: lax.all_gather(part, axis), value)  52.5 us
    mul x64, local copies, waits for them, and re-layouts, join_backward(): decay_late[:, None, :] * state_early + state_late  45 us
    dynamic_slice x64, local copies, waits for them, and re-layouts, step(): new = combine(before, jax.tree.map(lambda part: part[at], everything))  37.4 us
    unnamed x74, local copies, waits for them, and re-layouts  34.1 us
  transfers between devices with their start and end apart: 3, of which 0 were waited for; matrix products, arithmetic and copies ran while one was open for 49% of the time, Pallas kernels for 0%

commit v1 on v0

v1 whole, which is shorter than its diff:
```python
import functools

import jax
import jax.numpy as jnp
from jax import lax
from jax.experimental import pallas as pl
from jax.experimental.pallas import tpu as pltpu
from jax.sharding import PartitionSpec as P

EPSILON = 1e-06
EXACT = lax.Precision.HIGHEST
F32 = jnp.float32
LANES = 128
HALF = 8
STEPS = 4


def exact_dot(a, b):
    return jnp.dot(a, b, precision=EXACT, preferred_element_type=F32)


def iota(shape, dim):
    return lax.broadcasted_iota(jnp.int32, shape, dim)


def get_rows(ref, per, row, base=0):
    if per >= HALF:
        return ref[row // per, base + row % per : base + row % per + HALF, :]
    parts = [ref[row // per + s, base : base + per, :] for s in range(HALF // per)]
    return jnp.concatenate(parts, axis=0)


def put_rows(ref, per, row, block, base=0):
    if per >= HALF:
        ref[row // per, base + row % per : base + row % per + HALF, :] = block
    else:
        for s in range(HALF // per):
            ref[row // per + s, base : base + per, :] = block[s * per : (s + 1) * per]


def member_sums(first, second, members):
    groups = LANES // members
    lane, slot = iota((LANES, LANES), 0), iota((LANES, LANES), 1)
    pick = (slot == lane // members).astype(F32)
    pick_two = (slot == groups + lane // members).astype(F32)
    return exact_dot(first, pick) + exact_dot(second, pick_two)


def state_kernel(dims, k_ref, v_ref, rate_ref, res_ref, u_ref, a_ref, r_ref, d_ref, send_ref, tab):
    tokens, tiles, modes, members, per = dims
    groups = LANES // members

    def expand(ref, out, fn):
        for j in range(tiles):
            g, lane = iota((ref.shape[1], LANES), 0), iota((ref.shape[1], LANES), 1)
            pick = (g == groups * j + lane // members).astype(F32)
            tab[pl.ds(j, modes, stride=tiles), :] = exact_dot(ref[...], pick)

    expand(res_ref, None, None)
    r_ref[...] = tab[...]
    expand(rate_ref, None, None)
    rate = jnp.exp(tab[...])
    a_ref[...] = jnp.exp(-rate)
    tab[...] = jnp.exp(-rate * float(tokens))
    for row in range(0, modes * tiles, HALF):
        put_rows(d_ref, per, row, tab[row : row + HALF, :])

    def fill(b, _):
        rows = pl.ds(pl.multiple_of(b * 16, 16), 16)
        for j in range(tiles):
            cols = slice(j * LANES, (j + 1) * LANES)
            u = k_ref[rows, cols].astype(F32) * v_ref[rows, cols].astype(F32)
            u_ref[pl.ds(b * 16 * tiles + j, 16, stride=tiles), :] = u
        return 0

    lax.fori_loop(0, tokens // 16, fill, 0)

    span = modes // 2
    zero = jnp.zeros((HALF, LANES), F32)
    for h in range(0, tiles, HALF):
        for first in range(0, modes, span):
            rows = [(first + i) * tiles + h for i in range(span)]
            a = [a_ref[row : row + HALF, :] for row in rows]

            def step(n, carry):
                hs, ms = carry
                for s in range(STEPS):
                    t = n * STEPS + s
                    u = u_ref[pl.ds(pl.multiple_of(t * tiles + h, HALF), HALF), :]
                    aged = [x * y for x, y in zip(a, hs)]
                    ms = [x * m + y for x, m, y in zip(a, ms, aged)]
                    hs = [y + u for y in aged]
                return tuple(hs), tuple(ms)

            hs, ms = lax.fori_loop(0, tokens // STEPS, step, ((zero,) * span, (zero,) * span))
            for i, row in enumerate(rows):
                put_rows(send_ref, per, row, hs[i])
                put_rows(send_ref, per, row, ms[i], base=per)


def prefix_kernel(per, got_ref, d_ref, both_ref, send_ref):
    count = got_ref.shape[0]
    decay = d_ref[lax.axis_index("ctx")]
    decay = jnp.concatenate([decay, decay], axis=0)

    def step(i, before):
        both_ref[i] = before
        send_ref[i] = before[:per]
        return decay * before + got_ref[i]

    lax.fori_loop(0, count, step, jnp.zeros(decay.shape, F32), unroll=8)


def mix_kernel(
    dims, u_ref, gate_ref, cot_ref, skip_ref, gain_ref, a_ref, r_ref, in_ref, mixed_ref, sums_ref, y_ref, acc_ref
):
    tokens, tiles, modes, members, per = dims
    for h in range(0, tiles, HALF):
        rows = [i * tiles + h for i in range(modes)]
        a = [a_ref[row : row + HALF, :] for row in rows]
        res = [r_ref[row : row + HALF, :] for row in rows]

        def step(n, hs):
            for s in range(STEPS):
                at = pl.ds(pl.multiple_of((n * STEPS + s) * tiles + h, HALF), HALF)
                u = u_ref[at, :]
                hs = [x * y + u for x, y in zip(a, hs)]
                y = [x * z for x, z in zip(res, hs)]
                while len(y) > 1:
                    y = [y[i] + y[i + 1] for i in range(0, len(y), 2)]
                y_ref[at, :] = y[0]
            return tuple(hs)

        start = tuple(get_rows(in_ref, per, row) for row in rows)
        lax.fori_loop(0, tokens // STEPS, step, start)

    def block(b, _):
        rows = pl.ds(pl.multiple_of(b * 16, 16), 16)
        squares = jnp.zeros((16, LANES), F32)
        inner = jnp.zeros((16, LANES), F32)
        for j in range(tiles):
            cols = slice(j * LANES, (j + 1) * LANES)
            at = pl.ds(b * 16 * tiles + j, 16, stride=tiles)
            mixed = y_ref[at, :] + skip_ref[:, cols] * u_ref[at, :]
            mixed_ref[rows, cols] = mixed
            premix = gate_ref[rows, cols].astype(F32) * mixed
            pull = cot_ref[rows, cols].astype(F32) * gain_ref[:, cols]
            squares = squares + premix * premix
            inner = inner + pull * premix
        acc_ref[0, rows, :] = squares
        acc_ref[1, rows, :] = inner
        return 0

    lax.fori_loop(0, tokens // 16, block, 0)
    for s in range(2):
        sums_ref[s : s + 1, :] = jnp.sum(acc_ref[s].T, axis=0, keepdims=True)


def norm_kernel(
    dims, width, sums_ref, mixed_ref, u_ref, gate_ref, cot_ref, gain_ref, a_ref, in_ref,
    out_ref, grad_q_ref, w_ref, send_ref, row_ref, part_ref,
):
    tokens, tiles, modes, members, per = dims
    total = jnp.sum(sums_ref[...], axis=0)
    inverse = lax.rsqrt(total[0:1] / width + EPSILON)
    inner = inverse * total[1:2] / width
    row_ref[0] = jnp.broadcast_to(inverse, (LANES, tokens)).T
    row_ref[1] = jnp.broadcast_to(inner, (LANES, tokens)).T

    def block(b, _):
        rows = pl.ds(pl.multiple_of(b * 16, 16), 16)
        inverse, inner = row_ref[0, rows, :], row_ref[1, rows, :]
        for j in range(tiles):
            cols = slice(j * LANES, (j + 1) * LANES)
            mixed = mixed_ref[rows, cols]
            gate = gate_ref[rows, cols].astype(F32)
            gain = gain_ref[:, cols]
            normed = gate * mixed * inverse
            out_ref[rows, cols] = (normed * gain).astype(jnp.bfloat16)
            pull = cot_ref[rows, cols].astype(F32) * gain
            dpre = (pull - normed * inner) * inverse
            grad_q_ref[rows, cols] = (dpre * mixed).astype(jnp.bfloat16)
            w_ref[pl.ds(b * 16 * tiles + j, 16, stride=tiles), :] = dpre * gate
        return 0

    lax.fori_loop(0, tokens // 16, block, 0)

    span = modes // 2
    zero = jnp.zeros((HALF, LANES), F32)
    for h in range(0, tiles, HALF):
        for first in range(0, modes, span):
            rows = [(first + i) * tiles + h for i in range(span)]
            a = [a_ref[row : row + HALF, :] for row in rows]

            def step(n, carry):
                xs, ms, res, mom = carry
                for s in range(STEPS):
                    t = tokens - 1 - (n * STEPS + s)
                    at = pl.ds(pl.multiple_of(t * tiles + h, HALF), HALF)
                    w, u = w_ref[at, :], u_ref[at, :]
                    bs = [x + w for x in xs]
                    ms = [y * m + x for y, m, x in zip(a, ms, xs)]
                    xs = [y * b for y, b in zip(a, bs)]
                    res = [p + u * b for p, b in zip(res, bs)]
                    mom = [p + u * m for p, m in zip(mom, ms)]
                return tuple(xs), tuple(ms), tuple(res), tuple(mom)

            xs, ms, res, mom = lax.fori_loop(0, tokens // STEPS, step, ((zero,) * span,) * 4)
            for i, row in enumerate(rows):
                put_rows(send_ref, per, row, xs[i])
                part_ref[0, row : row + HALF, :] = res[i]
                lead_moment = a[i] * ms[i] + xs[i]
                part_ref[1, row : row + HALF, :] = mom[i] + lead_moment * get_rows(in_ref, per, row)
    part_ref[0] = member_sums(part_ref[0], part_ref[1], members)
    for row in range(0, modes * tiles, HALF):
        put_rows(send_ref, per, row, part_ref[0, row : row + HALF, :], base=per)


def suffix_kernel(dims, got_ref, both_ref, d_ref, send_ref):
    tokens, tiles, modes, members, per = dims
    count = got_ref.shape[0]
    decay = d_ref[lax.axis_index("ctx")]
    zero = jnp.zeros((per, LANES), F32)

    def step(n, carry):
        after, part, res, mom = carry
        i = count - 1 - n
        got, both = got_ref[i], both_ref[i]
        lead, before, moment = got[:per], both[:per], both[per:]
        send_ref[i, :per, :] = after
        aged = decay * after
        part = part + got[per:]
        res = res + lead * before
        mom = mom + lead * moment + float(tokens) * aged * before
        return aged + lead, part, res, mom

    _, part, res, mom = lax.fori_loop(0, count, step, (zero,) * 4, unroll=8)
    pad = max(HALF - per, 0)
    if pad:
        fill = jnp.zeros((pad, LANES), F32)
        res, mom = jnp.concatenate([res, fill], axis=0), jnp.concatenate([mom, fill], axis=0)
    part = part + member_sums(res, mom, members)[:per]

    def spread(i, _):
        send_ref[i, per:, :] = part
        return 0

    lax.fori_loop(0, count, spread, 0, unroll=8)


def grad_kernel(
    dims, total_tokens, got_ref, w_ref, k_ref, v_ref, skip_ref, a_ref, r_ref, residue_ref, log_ref,
    grad_k_ref, grad_v_ref, grad_res_ref, grad_log_ref, y_ref, tot_ref,
):
    tokens, tiles, modes, members, per = dims
    for h in range(0, tiles, HALF):
        rows = [i * tiles + h for i in range(modes)]
        a = [a_ref[row : row + HALF, :] for row in rows]
        res = [r_ref[row : row + HALF, :] for row in rows]

        def step(n, xs):
            for s in range(STEPS):
                t = tokens - 1 - (n * STEPS + s)
                at = pl.ds(pl.multiple_of(t * tiles + h, HALF), HALF)
                w = w_ref[at, :]
                bs = [x + w for x in xs]
                xs = [y * b for y, b in zip(a, bs)]
                y = [x * z for x, z in zip(res, bs)]
                while len(y) > 1:
                    y = [y[i] + y[i + 1] for i in range(0, len(y), 2)]
                y_ref[at, :] = y[0]
            return tuple(xs)

        start = tuple(get_rows(got_ref, per, row) for row in rows)
        lax.fori_loop(0, tokens // STEPS, step, start)

    def block(b, _):
        rows = pl.ds(pl.multiple_of(b * 16, 16), 16)
        for j in range(tiles):
            cols = slice(j * LANES, (j + 1) * LANES)
            at = pl.ds(b * 16 * tiles + j, 16, stride=tiles)
            grad = y_ref[at, :] + skip_ref[:, cols] * w_ref[at, :]
            grad_k_ref[rows, cols] = (grad * v_ref[rows, cols].astype(F32)).astype(jnp.bfloat16)
            grad_v_ref[rows, cols] = (grad * k_ref[rows, cols].astype(F32)).astype(jnp.bfloat16)
        return 0

    lax.fori_loop(0, tokens // 16, block, 0)

    for row in range(0, modes * tiles, HALF):
        tot_ref[row : row + HALF, :] = get_rows(got_ref, per, row, base=per)
    group_tile = LANES // members
    states, groups = modes * tiles, residue_ref.shape[0]
    slot, group = iota((LANES, groups), 0), iota((LANES, groups), 1)
    own = iota((states, groups), 0) % tiles == iota((states, groups), 1) // group_tile
    mode_of = (iota((LANES, states), 1) // tiles == iota((LANES, states), 0)).astype(F32)
    sums = []
    for s in range(2):
        pick = (slot == s * group_tile + group % group_tile).astype(F32)
        spread = jnp.where(own, exact_dot(tot_ref[...], pick), 0.0)
        sums.append(exact_dot(mode_of, spread).T[:, :modes] / total_tokens)
    grad_res_ref[...] = sums[0]
    grad_log_ref[...] = -residue_ref[...] * jnp.exp(log_ref[...]) * sums[1]


def call(kernel, name, outs, scratch=()):
    vmem = pl.BlockSpec(memory_space=pltpu.VMEM)
    return lambda *args: pl.pallas_call(
        kernel,
        name=name,
        out_shape=[jax.ShapeDtypeStruct(s, d) for s, d in outs],
        in_specs=[vmem] * len(args),
        out_specs=[vmem] * len(outs),
        scratch_shapes=[pltpu.VMEM(s, F32) for s in scratch],
    )(*args)


def per_device(out_gate, key_proj, value_proj, residue, log_decay, skip, gain, cotangent):
    tokens, channels = out_gate.shape
    groups, modes = residue.shape
    members, tiles = channels // groups, channels // LANES
    shards = lax.axis_size("ctx")
    width = float(channels * lax.axis_size("tp"))
    states = modes * tiles
    per = states // shards
    dims = (tokens, tiles, modes, members, per)
    bf16 = jnp.bfloat16
    flat, state = ((tokens * tiles, LANES), F32), ((states, LANES), F32)
    one, two = ((shards, per, LANES), F32), ((shards, 2 * per, LANES), F32)
    narrow = ((tokens, channels), bf16)
    skip, gain = skip[None], gain[None]

    def exchange(value):
        return lax.all_to_all(value, "ctx", 0, 0, tiled=True)

    u, a, r, d, send = call(
        functools.partial(state_kernel, dims), "state", [flat, state, state, one, two], [state[0]]
    )(key_proj, value_proj, log_decay.T, residue.T)
    both, send = call(functools.partial(prefix_kernel, per), "prefix", [two, one])(exchange(send), d)
    before = exchange(send)
    mixed, sums = call(
        functools.partial(mix_kernel, dims),
        "mix",
        [((tokens, channels), F32), ((2, tokens), F32)],
        [flat[0], (2, tokens, LANES)],
    )(u, out_gate, cotangent, skip, gain, a, r, before)
    sums = lax.all_gather(sums, "tp")
    mixer_out, grad_q, w, send = call(
        functools.partial(norm_kernel, dims, width),
        "norm",
        [narrow, narrow, flat, two],
        [(2, tokens, LANES), (2, states, LANES)],
    )(sums, mixed, u, out_gate, cotangent, gain, a, before)
    (send,) = call(functools.partial(suffix_kernel, dims), "suffix", [two])(exchange(send), both, d)
    grad_k, grad_v, grad_residue, grad_log_decay = call(
        functools.partial(grad_kernel, dims, float(tokens * shards)),
        "grad",
        [narrow, narrow, ((groups, modes), F32), ((groups, modes), F32)],
        [flat[0], state[0]],
    )(exchange(send), w, key_proj, value_proj, skip, a, r, residue, log_decay)
    return (mixer_out, grad_q, grad_k, grad_v, grad_residue, grad_log_decay)


def solution(mesh):
    tokens, split = P("ctx", "tp"), P("tp", None)
    return jax.shard_map(
        per_device,
        mesh=mesh,
        in_specs=(tokens, tokens, tokens, split, split, P("tp"), P("tp"), tokens),
        out_specs=(tokens, tokens, tokens, tokens, split, split),
        check_vma=False,
    )
```

time: 1500 us -> 125 us (0.08); the launches traced: 1470 us -> 125 us
  local copies, waits for them, and re-layouts: 747 us -> 5.04 us
  blocking collectives: 440 us -> 69.1 us
  other arithmetic: 193 us -> 0 us
  matrix products: 72.7 us -> 0 us
  Pallas kernels: 0 us -> 33.3 us
    gather x644 -> x0, local copies, waits for them, and re-layouts: 578 us -> none
    psum x3 -> x0, blocking collectives: 260 us -> none  [the longest x1 245 us: per_device(): lax.psum((residue_part.T, moment_part.T), 'ctx')]
    select_n x132 -> x0, other arithmetic: 174 us -> none  [the longest x128 174 us: step(): return jax.tree.map(lambda a, b: jnp.where(reached, a, b), new, before)]
    unnamed x1 -> x0, blocking collectives: 128 us -> none
    dot_general x19 -> x0, matrix products: 72.7 us -> none  [the longest x4 22.3 us: per_device(): jnp.einsum('tsg,nscg->ntcg', matrix, sub_signal, precision=HIGHEST_ACCURACY)]
    all_to_all x0 -> x3, blocking collectives: none -> 60.9 us  [exchange(): return lax.all_to_all(value, 'ctx', 0, 0, tiled=True)]
    mul x128 -> x0, local copies, waits for them, and re-layouts: 45.1 us -> none  [the longest x64 45 us: join_backward(): decay_late[:, None, :] * state_early + state_late]
    all_gather x1, blocking collectives: 52.5 us -> 8.23 us  [per_device(): sums = lax.all_gather(sums, 'tp')]
  transfers between devices with their start and end apart: 3 -> 1, of which waited for: 0 -> 1; matrix products, arithmetic and copies ran while one was open for 49% -> 1% of each run, Pallas kernels for 0% -> 0%
where the time goes in v1:
time: 125 us
  blocking collectives  69.1 us (55%)
  Pallas kernels  33.3 us (27%)
  waiting for transfers between devices  10.5 us (8%)
  starting transfers between devices  6.24 us (5%)
  local copies, waits for them, and re-layouts  5.04 us (4%)
    all_to_all x3, blocking collectives, exchange(): return lax.all_to_all(value, 'ctx', 0, 0, tiled=True)  60.9 us
    pallas_call x6, Pallas kernels, call(): pl.pallas_call(kernel, name=name, out_shape=[jax.ShapeDtypeStruct(s, d) f...  33.3 us
    all_to_all x1, waiting for transfers between devices, exchange(): return lax.all_to_all(value, 'ctx', 0, 0, tiled=True)  10.5 us
    all_gather x1, blocking collectives, per_device(): sums = lax.all_gather(sums, 'tp')  8.23 us
    all_to_all x1, starting transfers between devices, exchange(): return lax.all_to_all(value, 'ctx', 0, 0, tiled=True)  6.24 us
    unnamed x14, local copies, waits for them, and re-layouts  5.04 us
  transfers between devices with their start and end apart: 1, of which 1 were waited for; matrix products, arithmetic and copies ran while one was open for 1% of the time, Pallas kernels for 0%

profile of v1, /device:TPU:1, one launch (start us, length us, event | category | flops | bytes accessed | tf_op | source)
XLA Modules:
  0.0 124.9 jit_solution(2470817152304051300)
XLA Ops:
  0.6 7.1 %state.1 = (f32[2048,128]{1,0:T(8,128)}, f32[256,128]{1,0:T(8,128)}, f32[256,128]{1,0:T(8,128)}, f32[64,4,128]{2,1,0:T(4,128)}, f32[64,8,128]{2,1,0:T(8,128)}) custom-call(bf16[128,2048]{1,0:T(8,128)(2,1)} %k_ref.3, bf16[128,2048]{1,0:T(8,128)(2,1)} %v_ref.3, f32[16,128]{1,0:T(8,128)} %bitcast.10, f32[16,128]{1,0:T(8,128)} %bitcast.9), custom_call_target="tpu_custom_call" | custom-call | tf_op jit(solution)/shard_map/state/pallas_call | solution.py:307
  7.7 25.0 %all_to_all.20.got_ref = f32[64,8,128]{2,1,0:T(8,128)} all-to-all(f32[64,8,128]{2,1,0:T(8,128)} %get-tuple-element.26), channel_id=1, replica_groups=mesh['ctx'=64,'tp'=4] {'ctx'}, dimensions={0} | all-to-all | bytes 524288 | tf_op jit(solution)/shard_map/all_to_all | solution.py:333
  32.8 1.9 %prefix.1 = (f32[64,8,128]{2,1,0:T(8,128)}, f32[64,4,128]{2,1,0:T(4,128)}) custom-call(f32[64,8,128]{2,1,0:T(8,128)} %all_to_all.20.got_ref, f32[64,4,128]{2,1,0:T(4,128)} %get-tuple-element.27.d_ref), custom_call_target="tpu_custom_call" | custom-call | tf_op jit(solution)/shard_map/prefix/pallas_call | solution.py:307
  34.6 16.5 %all_to_all.21.in_ref = f32[64,4,128]{2,1,0:T(4,128)} all-to-all(f32[64,4,128]{2,1,0:T(4,128)} %get-tuple-element.28), channel_id=1, replica_groups=mesh['ctx'=64,'tp'=4] {'ctx'}, dimensions={0} | all-to-all | bytes 262144 | tf_op jit(solution)/shard_map/all_to_all | solution.py:333
  51.1 5.8 %mix.1 = (f32[128,2048]{1,0:T(8,128)}, f32[2,128]{1,0:T(2,128)}) custom-call(f32[2048,128]{1,0:T(8,128)} %get-tuple-element.23.u_ref, bf16[128,2048]{1,0:T(8,128)(2,1)} %gate_ref.3, bf16[128,2048]{1,0:T(8,128)(2,1)} %cot_ref.3, f32[1,2048]{1,0:T(1,128)} %bitcast.7, f32[1,2048]{1,0:T(1,128)} %bitcast.5, f32[256,128]{1,0:T(8,128)} %get-tuple-element.24.a_ref, ...), custom_call_target="tpu_custom_call" | custom-call | tf_op jit(solution)/shard_map/mix/pallas_call | solution.py:307
  56.9 0.0 copy-start.4
  56.9 0.7 copy-done.4
  57.6 8.2 %all-gather.1.sums_ref = f32[4,2,128]{2,1,0:T(2,128)} all-gather(f32[1,2,128]{2,1,0:T(2,128)S(1)} %bitcast.11), channel_id=2, replica_groups=mesh['ctx'=64,'tp'=4] {'tp'}, dimensions={0}, use_global_device_ids=true | all-gather | bytes 5120 | tf_op jit(solution)/shard_map/all_gather | solution.py:346
  65.8 9.5 %norm.1 = (bf16[128,2048]{1,0:T(8,128)(2,1)}, bf16[128,2048]{1,0:T(8,128)(2,1)}, f32[2048,128]{1,0:T(8,128)}, f32[64,8,128]{2,1,0:T(8,128)}) custom-call(f32[4,2,128]{2,1,0:T(2,128)} %all-gather.1.sums_ref, f32[128,2048]{1,0:T(8,128)} %get-tuple-element.30.mixed_ref, f32[2048,128]{1,0:T(8,128)} %get-tuple-element.23.u_ref, bf16[128,2048]{1,0:T(8,128)(2,1)} %gate_ref.3, ...), custom_call_target="tpu_custom_call" | custom-call | tf_op jit(solution)/shard_map/norm/pallas_call | solution.py:307
  75.4 19.4 %all_to_all.22.got_ref = f32[64,8,128]{2,1,0:T(8,128)} all-to-all(f32[64,8,128]{2,1,0:T(8,128)} %get-tuple-element.33), channel_id=1, replica_groups=mesh['ctx'=64,'tp'=4] {'ctx'}, dimensions={0} | all-to-all | bytes 524288 | tf_op jit(solution)/shard_map/all_to_all | solution.py:333
  94.8 2.2 %suffix.1 = f32[64,8,128]{2,1,0:T(8,128)} custom-call(f32[64,8,128]{2,1,0:T(8,128)} %all_to_all.22.got_ref, f32[64,8,128]{2,1,0:T(8,128)} %get-tuple-element.34.both_ref, f32[64,4,128]{2,1,0:T(4,128)} %get-tuple-element.27.d_ref), custom_call_target="tpu_custom_call" | custom-call | tf_op jit(solution)/shard_map/suffix/pallas_call | solution.py:307
  97.0 0.0 copy-start.2
  97.0 6.2 %all-to-all-start.3 = ((f32[64,8,128]{2,1,0:T(8,128)}), f32[64,8,128]{2,1,0:T(8,128)S(1)}, u32[]{:S(2)}, u32[]{:S(2)}) async-start(f32[64,8,128]{2,1,0:T(8,128)} %suffix.1), calls=%async_computation.3 | async-start | bytes 524288 | tf_op jit(solution)/shard_map/all_to_all | solution.py:333
  103.2 0.0 copy-done.2
  103.2 0.0 copy-start.3
  103.2 0.7 copy.18.residue_ref
  104.0 0.0 copy-done.3
  104.0 0.7 copy.19.log_ref
  104.7 10.5 %all-to-all-done.3.got_ref = f32[64,8,128]{2,1,0:T(8,128)S(1)} async-done(((f32[64,8,128]{2,1,0:T(8,128)}), f32[64,8,128]{2,1,0:T(8,128)S(1)}, u32[]{:S(2)}, u32[]{:S(2)}) %all-to-all-start.3) | async-done | bytes 262176 | tf_op jit(solution)/shard_map/all_to_all | solution.py:333
  115.2 0.7 copy-done
  115.9 6.8 %grad.1 = (bf16[128,2048]{1,0:T(8,128)(2,1)}, bf16[128,2048]{1,0:T(8,128)(2,1)}, f32[128,16]{1,0:T(8,128)}, f32[128,16]{1,0:T(8,128)}) custom-call(f32[64,8,128]{2,1,0:T(8,128)} %copy-done, f32[2048,128]{1,0:T(8,128)} %get-tuple-element.35.w_ref, bf16[128,2048]{1,0:T(8,128)(2,1)} %k_ref.3, bf16[128,2048]{1,0:T(8,128)(2,1)} %v_ref.3, f32[1,2048]{1,0:T(1,128)} %bitcast.8, ...), custom_call_target="tpu_custom_call" | custom-call | tf_op jit(solution)/shard_map/grad/pallas_call | solution.py:307
  122.7 1.5 %copy.20 = f32[128,16]{0,1:T(8,128)} copy(f32[128,16]{1,0:T(8,128)} %get-tuple-element.50) | data formatting | bytes 16384
  124.2 0.0 copy-done.1
  124.2 0.7 copy.21
  (2 shorter events, 0.0 us)
Async XLA Ops:
  56.9 0.7 copy-start.4
  97.0 6.3 %copy-start.2 = (f32[128,16]{0,1:T(8,128)S(1)}, f32[128,16]{0,1:T(8,128)}, u32[]{:S(2)}) copy-start(f32[128,16]{0,1:T(8,128)} %param.11) | copy-start | bytes 24580
  97.0 18.2 %all-to-all-start.3 = ((f32[64,8,128]{2,1,0:T(8,128)}), f32[64,8,128]{2,1,0:T(8,128)S(1)}, u32[]{:S(2)}, u32[]{:S(2)}) async-start(f32[64,8,128]{2,1,0:T(8,128)} %suffix.1), calls=%async_computation.3 | async-start | bytes 524288 | tf_op jit(solution)/shard_map/all_to_all | solution.py:333
  103.2 0.7 copy-start.3
  115.2 0.7 copy-start
  122.7 1.5 %copy-start.1 = (f32[128,16]{1,0:T(8,128)S(1)}, f32[128,16]{1,0:T(8,128)}, u32[]{:S(2)}) copy-start(f32[128,16]{1,0:T(8,128)} %get-tuple-element.51) | copy-start | bytes 24580

commit v2 on v1

v2 whole, which is shorter than its diff:
```python
import functools

import jax
import jax.numpy as jnp
from jax import lax
from jax.experimental import pallas as pl
from jax.experimental.pallas import tpu as pltpu
from jax.sharding import PartitionSpec as P

EPSILON = 1e-06
F32 = jnp.float32
LANES = 128
HALF = 8
STEPS = 8
BLOCK = 16


def iota(shape, dim):
    return lax.broadcasted_iota(jnp.int32, shape, dim)


def get_rows(ref, per, row, base=0):
    if per >= HALF:
        return ref[row // per, base + row % per : base + row % per + HALF, :]
    parts = [ref[row // per + s, base : base + per, :] for s in range(HALF // per)]
    return jnp.concatenate(parts, axis=0)


def put_rows(ref, per, row, block, base=0):
    if per >= HALF:
        ref[row // per, base + row % per : base + row % per + HALF, :] = block
    else:
        for s in range(HALF // per):
            ref[row // per + s, base : base + per, :] = block[s * per : (s + 1) * per]


def member_sums(first, second, members):
    groups = LANES // members
    shift = 1
    while shift < members:
        first = first + pltpu.roll(first, LANES - shift, 1)
        second = second + pltpu.roll(second, LANES - shift, 1)
        shift *= 2
    lane = iota(first.shape, 1)
    at = (lane % groups) * members
    first = jnp.take_along_axis(first, at, axis=1)
    second = jnp.take_along_axis(second, at, axis=1)
    return jnp.where(lane < groups, first, second)


def expand(ref, out, tiles, members):
    modes = ref.shape[0]
    value = ref[...]
    lane = iota(value.shape, 1)
    for j in range(tiles):
        at = (LANES // members) * j + lane // members
        out[pl.ds(j, modes, stride=tiles), :] = jnp.take_along_axis(value, at, axis=1)


def tree_sum(parts):
    while len(parts) > 1:
        parts = [sum(parts[i : i + 2]) for i in range(0, len(parts), 2)]
    return parts[0]


def tile(t, tiles, h):
    return pl.ds(pl.multiple_of(t * tiles + h, HALF), HALF)


def build_powers(first, factor_ref, out_ref):
    for row in range(0, factor_ref.shape[0], HALF):
        factor = factor_ref[row : row + HALF, :]
        value = jnp.ones_like(factor) if first is None else first[row : row + HALF, :]
        for i in range(BLOCK + 1):
            out_ref[i, row : row + HALF, :] = value
            if i < BLOCK:
                value = value * factor


def block_power(a_ref, out_ref):
    for row in range(0, a_ref.shape[0], HALF):
        value, n = a_ref[row : row + HALF, :], 1
        while n < BLOCK:
            value, n = value * value, 2 * n
        out_ref[row : row + HALF, :] = value


def fetch(pairs, sem, base=0):
    copies = [pltpu.make_async_copy(a, b, sem.at[base + i]) for i, (a, b) in enumerate(pairs)]
    for copy in copies:
        copy.start()
    return copies


def send_part(send_ref, send_hbm, sem, dims, first, span):
    tokens, tiles, modes, members, per = dims
    pieces = pl.ds(first * tiles // per, span * tiles // per)
    return fetch([(send_ref.at[pieces], send_hbm.at[pieces])], sem, first // span)


def state_kernel(
    dims, k_hbm, v_hbm, log_hbm, u_ref, a_ref, d_ref, send_hbm,
    k_ref, v_ref, log_ref, tab, power_ref, send_ref, sem, out_sem,
):
    tokens, tiles, modes, members, per = dims
    chunks = 4
    size = tokens // chunks
    (pull,) = fetch([(log_hbm, log_ref)], sem)
    copies = []
    for c in range(chunks):
        rows = pl.ds(c * size, size)
        pairs = [(k_hbm.at[rows, :], k_ref.at[rows, :]), (v_hbm.at[rows, :], v_ref.at[rows, :])]
        copies.append(fetch(pairs, sem, 1 + 2 * c))
    pull.wait()
    expand(log_ref, tab, tiles, members)
    for row in range(0, modes * tiles, HALF):
        rate = jnp.exp(tab[row : row + HALF, :])
        a_ref[row : row + HALF, :] = jnp.exp(-rate)
        put_rows(d_ref, per, row, jnp.exp(-rate * float(tokens)))
    build_powers(None, a_ref, power_ref)

    def fill(b, _):
        rows = pl.ds(pl.multiple_of(b * 16, 16), 16)
        for j in range(tiles):
            cols = slice(j * LANES, (j + 1) * LANES)
            u = k_ref[rows, cols].astype(F32) * v_ref[rows, cols].astype(F32)
            u_ref[pl.ds(b * 16 * tiles + j, 16, stride=tiles), :] = u
        return 0

    for c, pair in enumerate(copies):
        for copy in pair:
            copy.wait()
        lax.fori_loop(c * size // 16, (c + 1) * size // 16, fill, 0)

    span = modes // 2
    zero = jnp.zeros((HALF, LANES), F32)
    out = []
    for first in range(0, modes, span):
        for h in range(0, tiles, HALF):
            rows = [(first + i) * tiles + h for i in range(span)]

            def step(n, carry):
                hs, ms = carry
                xs = mx = None
                for i in range(BLOCK):
                    u = u_ref[tile(n * BLOCK + i, tiles, h), :]
                    if i == BLOCK - 1:
                        xs = [x + u for x in xs]
                        break
                    now = [power_ref[BLOCK - 1 - i, row : row + HALF, :] * u for row in rows]
                    xs = now if xs is None else [x + y for x, y in zip(xs, now)]
                    mx = xs if mx is None else [m + x for m, x in zip(mx, xs)]
                ends = [power_ref[BLOCK, row : row + HALF, :] for row in rows]
                ms = [e * (m + BLOCK * y) + x for e, m, y, x in zip(ends, ms, hs, mx)]
                hs = [e * y + x for e, y, x in zip(ends, hs, xs)]
                return tuple(hs), tuple(ms)

            hs, ms = lax.fori_loop(0, tokens // BLOCK, step, ((zero,) * span, (zero,) * span))
            for i, row in enumerate(rows):
                put_rows(send_ref, per, row, hs[i])
                put_rows(send_ref, per, row, ms[i], base=per)
        out += send_part(send_ref, send_hbm, out_sem, dims, first, span)
    for copy in out:
        copy.wait()


def local_kernel(
    dims, u_ref, a_ref, res_ref, r_ref, u_hbm, y_hbm, start_hbm, moment_hbm, y_ref, start_ref, moment_ref, sem
):
    tokens, tiles, modes, members, per = dims
    copies = fetch([(u_ref, u_hbm)], sem)
    expand(res_ref, r_ref, tiles, members)
    span = modes // 2
    zero = jnp.zeros((HALF, LANES), F32)
    for h in range(0, tiles, HALF):
        for first in range(0, modes, span):
            rows = [(first + i) * tiles + h for i in range(span)]
            a = [a_ref[row : row + HALF, :] for row in rows]
            res = [r_ref[row : row + HALF, :] for row in rows]

            def step(n, carry):
                hs, ms = carry
                for i, row in enumerate(rows):
                    start_ref[n, row : row + HALF, :] = hs[i]
                    moment_ref[n, row : row + HALF, :] = ms[i]
                for s in range(BLOCK):
                    at = tile(n * BLOCK + s, tiles, h)
                    u = u_ref[at, :]
                    aged = [x * y for x, y in zip(a, hs)]
                    ms = [x * m + y for x, m, y in zip(a, ms, aged)]
                    hs = [y + u for y in aged]
                    y = tree_sum([x * z for x, z in zip(res, hs)])
                    y_ref[at, :] = y_ref[at, :] + y if first else y
                return tuple(hs), tuple(ms)

            lax.fori_loop(0, tokens // BLOCK, step, ((zero,) * span, (zero,) * span))
    copies += fetch([(y_ref, y_hbm), (start_ref, start_hbm), (moment_ref, moment_hbm)], sem, 1)
    for copy in copies:
        copy.wait()


def prefix_kernel(per, got_ref, d_ref, after_hbm, both_ref, send_ref):
    count = got_ref.shape[0]
    decay = d_ref[lax.axis_index("ctx")]
    decay = jnp.concatenate([decay, decay], axis=0)

    def step(i, before):
        both_ref[i] = before
        send_ref[i] = before[:per]
        return decay * before + got_ref[i]

    lax.fori_loop(0, count, step, jnp.zeros(decay.shape, F32), unroll=8)


def age_states(dims, in_ref, end_ref, aged_ref):
    tokens, tiles, modes, members, per = dims
    for row in range(0, modes * tiles, HALF):
        state = get_rows(in_ref, per, row)
        for n in range(tokens // BLOCK):
            aged_ref[n, row : row + HALF, :] = state
            if n + 1 < tokens // BLOCK:
                state = state * end_ref[row : row + HALF, :]


def add_arrived(dims, aged_ref, taps_ref, y_ref, forward):
    tokens, tiles, modes, members, per = dims
    for h in range(0, tiles, HALF):
        rows = [i * tiles + h for i in range(modes)]

        def step(i, _):
            taps = [taps_ref[i + 1 if forward else i, row : row + HALF, :] for row in rows]
            for n in range(tokens // BLOCK):
                t = n * BLOCK + i
                at = tile(t if forward else tokens - 1 - t, tiles, h)
                parts = [x * aged_ref[n, row : row + HALF, :] for x, row in zip(taps, rows)]
                y_ref[at, :] = y_ref[at, :] + tree_sum(parts)
            return 0

        lax.fori_loop(0, BLOCK, step, 0)


def mix_kernel(
    dims, local_hbm, u_ref, gate_hbm, cot_hbm, skip_hbm, gain_hbm, a_ref, r_ref, in_ref, mixed_ref, sums_ref,
    gate_ref, cot_ref, skip_ref, gain_ref, power_ref, taps_ref, aged_ref, y_ref, acc_ref, sem,
):
    tokens, tiles, modes, members, per = dims
    copies = fetch(
        [(local_hbm, y_ref), (gate_hbm, gate_ref), (cot_hbm, cot_ref), (skip_hbm, skip_ref), (gain_hbm, gain_ref)], sem
    )
    build_powers(r_ref, a_ref, taps_ref)
    block_power(a_ref, power_ref)
    age_states(dims, in_ref, power_ref, aged_ref)
    copies[0].wait()
    add_arrived(dims, aged_ref, taps_ref, y_ref, True)
    for copy in copies[1:]:
        copy.wait()

    def block(b, _):
        rows = pl.ds(pl.multiple_of(b * 16, 16), 16)
        squares = jnp.zeros((16, LANES), F32)
        inner = jnp.zeros((16, LANES), F32)
        for j in range(tiles):
            cols = slice(j * LANES, (j + 1) * LANES)
            at = pl.ds(b * 16 * tiles + j, 16, stride=tiles)
            mixed = y_ref[at, :] + skip_ref[:, cols] * u_ref[at, :]
            mixed_ref[rows, cols] = mixed
            premix = gate_ref[rows, cols].astype(F32) * mixed
            pull = cot_ref[rows, cols].astype(F32) * gain_ref[:, cols]
            squares = squares + premix * premix
            inner = inner + pull * premix
        acc_ref[0, rows, :] = squares
        acc_ref[1, rows, :] = inner
        return 0

    lax.fori_loop(0, tokens // 16, block, 0)
    for s in range(2):
        sums_ref[s : s + 1, :] = jnp.sum(acc_ref[s].T, axis=0, keepdims=True)


def norm_kernel(
    dims, width, sums_ref, mixed_ref, gate_ref, cot_ref, gain_ref, a_ref, in_ref, u_hbm, start_hbm, moment_hbm,
    w_ref, send_hbm, row_hbm, row_ref, send_ref, u_ref, start_ref, moment_ref, power_ref, aged_ref, part_ref, sem, out_sem,
):
    tokens, tiles, modes, members, per = dims
    copies = fetch([(u_hbm, u_ref), (start_hbm, start_ref), (moment_hbm, moment_ref)], sem)
    total = jnp.sum(sums_ref[...], axis=0)
    inverse = lax.rsqrt(total[0:1] / width + EPSILON)
    inner = inverse * total[1:2] / width
    row_ref[0] = jnp.broadcast_to(inverse, (LANES, tokens)).T
    row_ref[1] = jnp.broadcast_to(inner, (LANES, tokens)).T
    save = fetch([(row_ref, row_hbm)], out_sem, 2)

    def block(b, _):
        rows = pl.ds(pl.multiple_of(b * 16, 16), 16)
        inverse, inner = row_ref[0, rows, :], row_ref[1, rows, :]
        for j in range(tiles):
            cols = slice(j * LANES, (j + 1) * LANES)
            gate = gate_ref[rows, cols].astype(F32)
            normed = gate * mixed_ref[rows, cols] * inverse
            pull = cot_ref[rows, cols].astype(F32) * gain_ref[:, cols]
            dpre = (pull - normed * inner) * inverse
            w_ref[pl.ds(b * 16 * tiles + j, 16, stride=tiles), :] = dpre * gate
        return 0

    lax.fori_loop(0, tokens // 16, block, 0)

    build_powers(None, a_ref, power_ref)
    age_states(dims, in_ref, power_ref.at[BLOCK], aged_ref)
    copies[0].wait()

    blocks = tokens // BLOCK
    zero = jnp.zeros((HALF, LANES), F32)
    for h in range(0, tiles, HALF):

        def pairs(n, lags):
            lags = list(lags)
            us = []
            for i in range(BLOCK):
                at = tile(n * BLOCK + i, tiles, h)
                us.append(u_ref[at, :])
                w = w_ref[at, :]
                for lag in range(i + 1):
                    lags[lag] = lags[lag] + w * us[i - lag]
            return tuple(lags)

        lags = lax.fori_loop(0, blocks, pairs, (zero,) * BLOCK)
        scaled = [lag * float(i) for i, lag in enumerate(lags)]
        for r in range(modes):
            row = r * tiles + h
            decay = power_ref[1, row : row + HALF, :]
            first, second = lags[-1], scaled[-1]
            for i in range(BLOCK - 2, -1, -1):
                first = first * decay + lags[i]
                second = second * decay + scaled[i] if i else second * decay
            part_ref[0, row : row + HALF, :] = first
            part_ref[1, row : row + HALF, :] = second

    copies[1].wait()
    copies[2].wait()

    span = modes // 2
    out = []
    for first in range(0, modes, span):
        for h in range(0, tiles, HALF):
            rows = [(first + i) * tiles + h for i in range(span)]

            def step(m, carry):
                lead, res, mom = carry
                n = blocks - 1 - m
                xs = mx = None
                for i in range(BLOCK - 1, -1, -1):
                    w = w_ref[tile(n * BLOCK + i, tiles, h), :]
                    now = [power_ref[i + 1, row : row + HALF, :] * w for row in rows]
                    xs = now if xs is None else [x + y for x, y in zip(xs, now)]
                    mx = xs if mx is None else [x + y for x, y in zip(mx, xs)]
                aged = [aged_ref[n, row : row + HALF, :] for row in rows]
                states = [start_ref[n, row : row + HALF, :] + g for row, g in zip(rows, aged)]
                age = (n * BLOCK).astype(F32)
                moments = [moment_ref[n, row : row + HALF, :] + age * g for row, g in zip(rows, aged)]
                lead = [power_ref[BLOCK, row : row + HALF, :] * y + x for row, y, x in zip(rows, lead, xs)]
                res = [p + x * s for p, x, s in zip(res, xs, states)]
                mom = [p + y * s + x * t for p, y, s, x, t in zip(mom, mx, states, xs, moments)]
                return tuple(lead), tuple(res), tuple(mom)

            start = (
                (zero,) * span,
                tuple(part_ref[0, row : row + HALF, :] for row in rows),
                tuple(part_ref[1, row : row + HALF, :] for row in rows),
            )
            lead, res, mom = lax.fori_loop(0, blocks, step, start)
            for i, row in enumerate(rows):
                put_rows(send_ref, per, row, lead[i])
                put_rows(send_ref, per, row, member_sums(res[i], mom[i], members), base=per)
        out += send_part(send_ref, send_hbm, out_sem, dims, first, span)
    for copy in save + out:
        copy.wait()


def back_kernel(dims, row_ref, mixed_ref, gate_ref, cot_ref, gain_ref, w_ref, a_ref, r_ref, out_ref, grad_q_ref, y_ref):
    tokens, tiles, modes, members, per = dims

    def block(b, _):
        rows = pl.ds(pl.multiple_of(b * 16, 16), 16)
        inverse, inner = row_ref[0, rows, :], row_ref[1, rows, :]
        for j in range(tiles):
            cols = slice(j * LANES, (j + 1) * LANES)
            mixed = mixed_ref[rows, cols]
            gain = gain_ref[:, cols]
            normed = gate_ref[rows, cols].astype(F32) * mixed * inverse
            out_ref[rows, cols] = (normed * gain).astype(jnp.bfloat16)
            pull = cot_ref[rows, cols].astype(F32) * gain
            dpre = (pull - normed * inner) * inverse
            grad_q_ref[rows, cols] = (dpre * mixed).astype(jnp.bfloat16)
        return 0

    lax.fori_loop(0, tokens // 16, block, 0)
    zero = jnp.zeros((HALF, LANES), F32)
    for h in range(0, tiles, HALF):
        rows = [i * tiles + h for i in range(modes)]
        a = [a_ref[row : row + HALF, :] for row in rows]
        res = [r_ref[row : row + HALF, :] for row in rows]

        def step(n, xs):
            for s in range(STEPS):
                at = tile(tokens - 1 - (n * STEPS + s), tiles, h)
                w = w_ref[at, :]
                bs = [x + w for x in xs]
                xs = [y * b for y, b in zip(a, bs)]
                y_ref[at, :] = tree_sum([x * z for x, z in zip(res, bs)])
            return tuple(xs)

        lax.fori_loop(0, tokens // STEPS, step, (zero,) * modes)


def suffix_kernel(dims, got_ref, both_ref, d_ref, after_hbm, send_ref):
    tokens, tiles, modes, members, per = dims
    count = got_ref.shape[0]
    decay = d_ref[lax.axis_index("ctx")]
    zero = jnp.zeros((per, LANES), F32)

    def step(n, carry):
        after, part, mom = carry
        i = count - 1 - n
        got, both = got_ref[i], both_ref[i]
        lead, before, moment = got[:per], both[:per], both[per:]
        send_ref[i, :per, :] = after
        aged = decay * after
        part = part + got[per:]
        mom = mom + lead * moment + float(tokens) * aged * before
        return aged + lead, part, mom

    _, part, mom = lax.fori_loop(0, count, step, (zero,) * 3, unroll=8)
    pad = max(HALF - per, 0)
    if pad:
        mom = jnp.concatenate([mom, jnp.zeros((pad, LANES), F32)], axis=0)
    part = part + member_sums(jnp.zeros_like(mom), mom, members)[:per]

    def spread(i, _):
        send_ref[i, per:, :] = part
        return 0

    lax.fori_loop(0, count, spread, 0, unroll=8)


def grad_kernel(
    dims, total_tokens, got_ref, local_hbm, w_ref, k_hbm, v_hbm, skip_hbm, a_ref, r_ref, residue_hbm, log_hbm,
    grad_k_ref, grad_v_ref, grad_res_ref, grad_log_ref,
    k_ref, v_ref, skip_ref, residue_ref, log_ref, power_ref, taps_ref, aged_ref, y_ref, tot_ref, sem,
):
    tokens, tiles, modes, members, per = dims
    copies = fetch(
        [
            (local_hbm, y_ref), (k_hbm, k_ref), (v_hbm, v_ref), (skip_hbm, skip_ref),
            (residue_hbm, residue_ref), (log_hbm, log_ref),
        ],
        sem,
    )
    build_powers(r_ref, a_ref, taps_ref)
    block_power(a_ref, power_ref)
    age_states(dims, got_ref, power_ref, aged_ref)
    copies[0].wait()
    add_arrived(dims, aged_ref, taps_ref, y_ref, False)
    for copy in copies[1:]:
        copy.wait()

    def block(b, _):
        rows = pl.ds(pl.multiple_of(b * 16, 16), 16)
        for j in range(tiles):
            cols = slice(j * LANES, (j + 1) * LANES)
            at = pl.ds(b * 16 * tiles + j, 16, stride=tiles)
            grad = y_ref[at, :] + skip_ref[:, cols] * w_ref[at, :]
            grad_k_ref[rows, cols] = (grad * v_ref[rows, cols].astype(F32)).astype(jnp.bfloat16)
            grad_v_ref[rows, cols] = (grad * k_ref[rows, cols].astype(F32)).astype(jnp.bfloat16)
        return 0

    lax.fori_loop(0, tokens // 16, block, 0)

    for row in range(0, modes * tiles, HALF):
        tot_ref[row : row + HALF, :] = get_rows(got_ref, per, row, base=per)
    groups = LANES // members
    lane = iota((modes, LANES), 1)
    first = second = jnp.zeros((modes, LANES), F32)
    for j in range(tiles):
        value = tot_ref[pl.ds(j, modes, stride=tiles), :]
        own = lane // groups == j
        first = jnp.where(own, jnp.take_along_axis(value, lane % groups, axis=1), first)
        second = jnp.where(own, jnp.take_along_axis(value, groups + lane % groups, axis=1), second)
    grad_res_ref[...] = first / total_tokens
    grad_log_ref[...] = -residue_ref[...] * jnp.exp(log_ref[...]) * second / total_tokens


def call(kernel, name, outs, scratch=(), hbm=(), out_hbm=()):
    vmem, far = pl.BlockSpec(memory_space=pltpu.VMEM), pl.BlockSpec(memory_space=pltpu.HBM)

    def place(i, value):
        return pltpu.with_memory_space_constraint(value, pltpu.HBM) if i in hbm else value

    return lambda *args: pl.pallas_call(
        kernel,
        name=name,
        out_shape=[pltpu.HBM(s, d) if i in out_hbm else jax.ShapeDtypeStruct(s, d) for i, (s, d) in enumerate(outs)],
        in_specs=[far if i in hbm else vmem for i in range(len(args))],
        out_specs=[far if i in out_hbm else vmem for i in range(len(outs))],
        scratch_shapes=[pltpu.VMEM(*s) if isinstance(s, tuple) else s for s in scratch],
        compiler_params=pltpu.CompilerParams(vmem_limit_bytes=16 * 2**20),
    )(*(place(i, x) for i, x in enumerate(args)))


def per_device(out_gate, key_proj, value_proj, residue, log_decay, skip, gain, cotangent):
    tokens, channels = out_gate.shape
    groups, modes = residue.shape
    members, tiles = channels // groups, channels // LANES
    shards = lax.axis_size("ctx")
    width = float(channels * lax.axis_size("tp"))
    states = modes * tiles
    blocks = tokens // BLOCK
    per = states // shards
    dims = (tokens, tiles, modes, members, per)
    bf16 = jnp.bfloat16
    flat, state = ((tokens * tiles, LANES), F32), ((states, LANES), F32)
    powers, starts = ((BLOCK + 1, states, LANES), F32), ((blocks, states, LANES), F32)
    one, two = ((shards, per, LANES), F32), ((shards, 2 * per, LANES), F32)
    narrow, small = ((tokens, channels), bf16), ((modes, groups), F32)
    rows = ((2, tokens, LANES), F32)
    line = ((1, channels), F32)
    skip, gain = skip[None], gain[None]
    residue, log_decay = residue.T, log_decay.T

    def exchange(value):
        return lax.all_to_all(value, "ctx", 0, 0, tiled=True)

    def sems(n):
        return pltpu.SemaphoreType.DMA((n,))

    u, a, d, send = call(
        functools.partial(state_kernel, dims),
        "state",
        [flat, state, one, two],
        [narrow, narrow, small, state, powers, two, sems(9), sems(2)],
        hbm=(0, 1, 2),
        out_hbm=(3,),
    )(key_proj, value_proj, log_decay)
    got = exchange(send)
    r, far_u, local, start, moment = call(
        functools.partial(local_kernel, dims),
        "local",
        [state, flat, flat, starts, starts],
        [flat, starts, starts, sems(4)],
        out_hbm=(1, 2, 3, 4),
    )(u, a, residue)
    both, send = call(functools.partial(prefix_kernel, per), "prefix", [two, one], hbm=(2,))(got, d, start)
    before = exchange(send)
    mixed, sums = call(
        functools.partial(mix_kernel, dims),
        "mix",
        [((tokens, channels), F32), ((2, tokens), F32)],
        [narrow, narrow, line, line, state, powers, starts, flat, rows, sems(5)],
        hbm=(0, 2, 3, 4, 5),
    )(local, u, out_gate, cotangent, skip, gain, a, r, before)
    sums = lax.all_gather(sums, "tp")
    w, send, row = call(
        functools.partial(norm_kernel, dims, width),
        "norm",
        [flat, two, rows],
        [rows, two, flat, starts, starts, powers, starts, ((2, states, LANES), F32), sems(3), sems(3)],
        hbm=(7, 8, 9),
        out_hbm=(1, 2),
    )(sums, mixed, out_gate, cotangent, gain, a, before, far_u, start, moment)
    got = exchange(send)
    mixer_out, grad_q, local = call(functools.partial(back_kernel, dims), "back", [narrow, narrow, flat])(
        row, mixed, out_gate, cotangent, gain, w, a, r
    )
    (send,) = call(functools.partial(suffix_kernel, dims), "suffix", [two], hbm=(3,))(got, both, d, grad_q)
    grad_k, grad_v, grad_residue, grad_log_decay = call(
        functools.partial(grad_kernel, dims, float(tokens * shards)),
        "grad",
        [narrow, narrow, small, small],
        [narrow, narrow, line, small, small, state, powers, starts, flat, state, sems(6)],
        hbm=(1, 3, 4, 5, 8, 9),
    )(exchange(send), local, w, key_proj, value_proj, skip, a, r, residue, log_decay)
    return (mixer_out, grad_q, grad_k, grad_v, grad_residue.T, grad_log_decay.T)


def solution(mesh):
    tokens, split = P("ctx", "tp"), P("tp", None)
    return jax.shard_map(
        per_device,
        mesh=mesh,
        in_specs=(tokens, tokens, tokens, split, split, P("tp"), P("tp"), tokens),
        out_specs=(tokens, tokens, tokens, tokens, split, split),
        check_vma=False,
    )
```

time: 125 us -> 109 us (0.87)
  blocking collectives: 69.1 us -> 42 us
  starting transfers between devices: 6.24 us -> 20.3 us
  Pallas kernels: 33.3 us -> 29.8 us
  waiting for transfers between devices: 10.5 us -> 13 us
  local copies, waits for them, and re-layouts: 5.04 us -> 2.85 us
    all_to_all x3 -> x2, blocking collectives: 60.9 us -> 34 us  [exchange(): return lax.all_to_all(value, 'ctx', 0, 0, tiled=True)]
    all_to_all x1 -> x2, starting transfers between devices: 6.24 us -> 20.3 us  [exchange(): return lax.all_to_all(value, 'ctx', 0, 0, tiled=True)]
    pallas_call x6 -> x8, Pallas kernels: 33.3 us -> 29.8 us  [call(): pl.pallas_call(kernel, name=name, out_shape=[pltpu.HBM(s, d) if i in out_...]
    all_to_all x1 -> x2, waiting for transfers between devices: 10.5 us -> 13 us  [exchange(): return lax.all_to_all(value, 'ctx', 0, 0, tiled=True)]
    unnamed x14 -> x16, local copies, waits for them, and re-layouts: 5.04 us -> 2.85 us
  transfers between devices with their start and end apart: 1 -> 2, of which waited for: 1 -> 2; matrix products, arithmetic and copies ran while one was open for 1% -> 0% of each run, Pallas kernels for 0% -> 8%
where the time goes in v2:
time: 109 us
  blocking collectives  42 us (39%)
  Pallas kernels  29.8 us (27%)
  starting transfers between devices  20.3 us (19%)
  waiting for transfers between devices  13 us (12%)
  local copies, waits for them, and re-layouts  2.85 us (3%)
    all_to_all x2, blocking collectives, exchange(): return lax.all_to_all(value, 'ctx', 0, 0, tiled=True)  34 us
    pallas_call x8, Pallas kernels, call(): pl.pallas_call(kernel, name=name, out_shape=[pltpu.HBM(s, d) if i in out_...  29.8 us
    all_to_all x2, starting transfers between devices, exchange(): return lax.all_to_all(value, 'ctx', 0, 0, tiled=True)  20.3 us
    all_to_all x2, waiting for transfers between devices, exchange(): return lax.all_to_all(value, 'ctx', 0, 0, tiled=True)  13 us
    all_gather x1, blocking collectives, per_device(): sums = lax.all_gather(sums, 'tp')  7.97 us
    unnamed x16, local copies, waits for them, and re-layouts  2.85 us
  transfers between devices with their start and end apart: 2, of which 2 were waited for; matrix products, arithmetic and copies ran while one was open for 0% of the time, Pallas kernels for 8%

profile of v2, /device:TPU:1, one launch (start us, length us, event | category | flops | bytes accessed | tf_op | source)
XLA Modules:
  0.0 108.7 jit_solution(653683303735896254)
XLA Ops:
  0.6 4.0 %state.1 = (f32[2048,128]{1,0:T(8,128)S(1)}, f32[256,128]{1,0:T(8,128)S(1)}, f32[64,4,128]{2,1,0:T(4,128)S(1)}, f32[64,8,128]{2,1,0:T(8,128)}) custom-call(bf16[128,2048]{1,0:T(8,128)(2,1)} %k_hbm.3, bf16[128,2048]{1,0:T(8,128)(2,1)} %v_hbm.3, f32[16,128]{1,0:T(8,128)} %bitcast.13), custom_call_target="tpu_custom_call" | custom-call | tf_op jit(solution)/shard_map/state/pallas_call | solution.py:498
  4.6 0.0 copy-start.7
  4.6 13.0 %all-to-all-start = ((f32[64,8,128]{2,1,0:T(8,128)}), f32[64,8,128]{2,1,0:T(8,128)S(1)}, u32[]{:S(2)}, u32[]{:S(2)}) async-start(f32[64,8,128]{2,1,0:T(8,128)} %get-tuple-element.33), calls=%async_computation | async-start | bytes 524288 | tf_op jit(solution)/shard_map/all_to_all | solution.py:530
  17.6 0.0 copy-done.7
  17.7 5.2 %local.1 = (f32[256,128]{1,0:T(8,128)S(1)}, f32[2048,128]{1,0:T(8,128)}, f32[2048,128]{1,0:T(8,128)}, f32[8,256,128]{2,1,0:T(8,128)}, f32[8,256,128]{2,1,0:T(8,128)}) custom-call(f32[2048,128]{1,0:T(8,128)S(1)} %get-tuple-element.29.u_ref, f32[256,128]{1,0:T(8,128)S(1)} %get-tuple-element.30.a_ref, f32[16,128]{1,0:T(8,128)S(1)} %bitcast.11), custom_call_target="tpu_custom_call" | custom-call | tf_op jit(solution)/shard_map/local/pallas_call | solution.py:498
  22.8 6.8 %all-to-all-done.got_ref = f32[64,8,128]{2,1,0:T(8,128)S(1)} async-done(((f32[64,8,128]{2,1,0:T(8,128)}), f32[64,8,128]{2,1,0:T(8,128)S(1)}, u32[]{:S(2)}, u32[]{:S(2)}) %all-to-all-start) | async-done | bytes 262176 | tf_op jit(solution)/shard_map/all_to_all | solution.py:530
  29.6 0.1 prefix.1
  29.8 16.2 %all_to_all.20.in_ref = f32[64,4,128]{2,1,0:T(4,128)S(1)} all-to-all(f32[64,4,128]{2,1,0:T(4,128)S(1)} %get-tuple-element.36), channel_id=1, replica_groups=mesh['ctx'=64,'tp'=4] {'ctx'}, dimensions={0} | all-to-all | bytes 262144 | tf_op jit(solution)/shard_map/all_to_all | solution.py:530
  45.9 3.9 %mix.1 = (f32[128,2048]{1,0:T(8,128)S(1)}, f32[2,128]{1,0:T(2,128)S(1)}) custom-call(f32[2048,128]{1,0:T(8,128)} %get-tuple-element.31.local_hbm, f32[2048,128]{1,0:T(8,128)S(1)} %get-tuple-element.29.u_ref, bf16[128,2048]{1,0:T(8,128)(2,1)} %gate_ref.3, bf16[128,2048]{1,0:T(8,128)(2,1)} %cot_ref.3, f32[1,2048]{1,0:T(1,128)} %bitcast.15, f32[1,2048]{1,0:T(1,128)} %bitcast.7, ...), custom_call_target="tpu_custom_call" | custom-call | tf_op jit(solution)/shard_map/mix/pallas_call | solution.py:498
  49.8 0.0 copy-done.3
  49.8 0.0 copy-start.6
  49.8 8.0 %all-gather.1.sums_ref = f32[4,2,128]{2,1,0:T(2,128)S(1)} all-gather(f32[1,2,128]{2,1,0:T(2,128)S(1)} %bitcast.12), channel_id=2, replica_groups=mesh['ctx'=64,'tp'=4] {'tp'}, dimensions={0}, use_global_device_ids=true | all-gather | bytes 5120 | tf_op jit(solution)/shard_map/all_gather | solution.py:560
  57.8 0.0 copy-done
  57.8 6.6 %norm.1 = (f32[2048,128]{1,0:T(8,128)S(1)}, f32[64,8,128]{2,1,0:T(8,128)}, f32[2,128,128]{2,1,0:T(8,128)}) custom-call(f32[4,2,128]{2,1,0:T(2,128)S(1)} %all-gather.1.sums_ref, f32[128,2048]{1,0:T(8,128)S(1)} %get-tuple-element.38.mixed_ref, bf16[128,2048]{1,0:T(8,128)(2,1)S(1)} %copy-done, bf16[128,2048]{1,0:T(8,128)(2,1)S(1)} %copy-done.1, ...), custom_call_target="tpu_custom_call" | custom-call | tf_op jit(solution)/shard_map/norm/pallas_call | solution.py:498
  64.4 7.3 %all-to-all-start.2 = ((f32[64,8,128]{2,1,0:T(8,128)}), f32[64,8,128]{2,1,0:T(8,128)}, u32[]{:S(2)}, u32[]{:S(2)}) async-start(f32[64,8,128]{2,1,0:T(8,128)} %get-tuple-element.45), calls=%async_computation.2 | async-start | bytes 524288 | tf_op jit(solution)/shard_map/all_to_all | solution.py:530
  71.7 0.0 copy-start.5
  71.7 0.9 copy-done.5
  72.6 3.8 %back.1 = (bf16[128,2048]{1,0:T(8,128)(2,1)}, bf16[128,2048]{1,0:T(8,128)(2,1)}, f32[2048,128]{1,0:T(8,128)S(1)}) custom-call(f32[2,128,128]{2,1,0:T(8,128)S(1)} %copy-done.5, f32[128,2048]{1,0:T(8,128)S(1)} %get-tuple-element.38.mixed_ref, bf16[128,2048]{1,0:T(8,128)(2,1)S(1)} %copy-done, bf16[128,2048]{1,0:T(8,128)(2,1)S(1)} %copy-done.1, ...), custom_call_target="tpu_custom_call" | custom-call | tf_op jit(solution)/shard_map/back/pallas_call | solution.py:498
  76.4 1.0 copy-done.2
  77.4 6.2 %all-to-all-done.2.got_ref = f32[64,8,128]{2,1,0:T(8,128)} async-done(((f32[64,8,128]{2,1,0:T(8,128)}), f32[64,8,128]{2,1,0:T(8,128)}, u32[]{:S(2)}, u32[]{:S(2)}) %all-to-all-start.2) | async-done | bytes 262176 | tf_op jit(solution)/shard_map/all_to_all | solution.py:530
  83.6 0.9 copy-done.4
  84.6 1.5 %suffix.1 = f32[64,8,128]{2,1,0:T(8,128)S(1)} custom-call(f32[64,8,128]{2,1,0:T(8,128)} %all-to-all-done.2.got_ref, f32[64,8,128]{2,1,0:T(8,128)S(1)} %copy-done.4, f32[64,4,128]{2,1,0:T(4,128)S(1)} %get-tuple-element.34.d_ref, bf16[128,2048]{1,0:T(8,128)(2,1)} %get-tuple-element.24.after_hbm), custom_call_target="tpu_custom_call" | custom-call | tf_op jit(solution)/shard_map/suffix/pallas_call | solution.py:498
  86.1 17.9 %all_to_all.21.got_ref = f32[64,8,128]{2,1,0:T(8,128)S(1)} all-to-all(f32[64,8,128]{2,1,0:T(8,128)S(1)} %suffix.1), channel_id=1, replica_groups=mesh['ctx'=64,'tp'=4] {'ctx'}, dimensions={0} | all-to-all | bytes 524288 | tf_op jit(solution)/shard_map/all_to_all | solution.py:530
  104.0 4.7 %grad.1 = (bf16[128,2048]{1,0:T(8,128)(2,1)}, bf16[128,2048]{1,0:T(8,128)(2,1)}, f32[16,128]{1,0:T(8,128)}, f32[16,128]{1,0:T(8,128)}) custom-call(f32[64,8,128]{2,1,0:T(8,128)S(1)} %all_to_all.21.got_ref, f32[2048,128]{1,0:T(8,128)} %copy-done.2, f32[2048,128]{1,0:T(8,128)S(1)} %get-tuple-element.42.w_ref, bf16[128,2048]{1,0:T(8,128)(2,1)} %k_hbm.3, ...), custom_call_target="tpu_custom_call" | custom-call | tf_op jit(solution)/shard_map/grad/pallas_call | solution.py:498
  (7 shorter events, 0.0 us)
Async XLA Ops:
  4.6 13.0 %copy-start.7 = (f32[128,16]{0,1:T(8,128)S(1)}, f32[128,16]{0,1:T(8,128)}, u32[]{:S(2)}) copy-start(f32[128,16]{0,1:T(8,128)} %param.11) | copy-start | bytes 24580
  4.6 25.0 %all-to-all-start = ((f32[64,8,128]{2,1,0:T(8,128)}), f32[64,8,128]{2,1,0:T(8,128)S(1)}, u32[]{:S(2)}, u32[]{:S(2)}) async-start(f32[64,8,128]{2,1,0:T(8,128)} %get-tuple-element.33), calls=%async_computation | async-start | bytes 524288 | tf_op jit(solution)/shard_map/all_to_all | solution.py:530
  29.7 20.1 %copy-start.3 = (f32[64,8,128]{2,1,0:T(8,128)}, f32[64,8,128]{2,1,0:T(8,128)S(1)}, u32[]{:S(2)}) copy-start(f32[64,8,128]{2,1,0:T(8,128)S(1)} %get-tuple-element.46.both_ref) | copy-start | bytes 786436
  45.9 11.9 %copy-start = (bf16[128,2048]{1,0:T(8,128)(2,1)S(1)}, bf16[128,2048]{1,0:T(8,128)(2,1)}, u32[]{:S(2)}) copy-start(bf16[128,2048]{1,0:T(8,128)(2,1)} %gate_ref.3) | copy-start | bytes 1572868
  45.9 11.9 %copy-start.1 = (bf16[128,2048]{1,0:T(8,128)(2,1)S(1)}, bf16[128,2048]{1,0:T(8,128)(2,1)}, u32[]{:S(2)}) copy-start(bf16[128,2048]{1,0:T(8,128)(2,1)} %cot_ref.3) | copy-start | bytes 1572868
  49.8 8.0 %copy-start.6 = (f32[2048]{0:T(1024)S(1)}, f32[2048]{0:T(1024)}, u32[]{:S(2)}) copy-start(f32[2048]{0:T(1024)} %param.14) | copy-start | bytes 24580
  64.4 19.2 %all-to-all-start.2 = ((f32[64,8,128]{2,1,0:T(8,128)}), f32[64,8,128]{2,1,0:T(8,128)}, u32[]{:S(2)}, u32[]{:S(2)}) async-start(f32[64,8,128]{2,1,0:T(8,128)} %get-tuple-element.45), calls=%async_computation.2 | async-start | bytes 524288 | tf_op jit(solution)/shard_map/all_to_all | solution.py:530
  71.7 0.9 copy-start.5
  76.4 1.0 copy-start.2
  83.6 1.0 copy-start.4

commit v3 on v2

--- a/solution.py
+++ b/solution.py
@@ -34,18 +34,20 @@
             ref[row // per + s, base : base + per, :] = block[s * per : (s + 1) * per]
 
 
-def member_sums(first, second, members):
+def member_sums(first, second, members, per):
     groups = LANES // members
     shift = 1
     while shift < members:
         first = first + pltpu.roll(first, LANES - shift, 1)
         second = second + pltpu.roll(second, LANES - shift, 1)
         shift *= 2
-    lane = iota(first.shape, 1)
+    row, lane = iota(first.shape, 0), iota(first.shape, 1)
     at = (lane % groups) * members
     first = jnp.take_along_axis(first, at, axis=1)
     second = jnp.take_along_axis(second, at, axis=1)
-    return jnp.where(lane < groups, first, second)
+    value = jnp.where((lane // groups) % 2 == 0, first, second)
+    value = jnp.where(lane // (2 * groups) == row % per, value, 0.0)
+    return [jnp.sum(value[i : i + per], axis=0, keepdims=True) for i in range(0, first.shape[0], per)]
 
 
 def expand(ref, out, tiles, members):
@@ -165,7 +167,7 @@
 
 
 def local_kernel(
-    dims, u_ref, a_ref, res_ref, r_ref, u_hbm, y_hbm, start_hbm, moment_hbm, y_ref, start_ref, moment_ref, sem
+    dims, u_ref, a_ref, res_ref, skip_ref, r_ref, u_hbm, y_hbm, start_hbm, moment_hbm, y_ref, start_ref, moment_ref, sem
 ):
     tokens, tiles, modes, members, per = dims
     copies = fetch([(u_ref, u_hbm)], sem)
@@ -177,6 +179,7 @@
             rows = [(first + i) * tiles + h for i in range(span)]
             a = [a_ref[row : row + HALF, :] for row in rows]
             res = [r_ref[row : row + HALF, :] for row in rows]
+            skip = skip_ref[h : h + HALF, :]
 
             def step(n, carry):
                 hs, ms = carry
@@ -190,7 +193,7 @@
                     ms = [x * m + y for x, m, y in zip(a, ms, aged)]
                     hs = [y + u for y in aged]
                     y = tree_sum([x * z for x, z in zip(res, hs)])
-                    y_ref[at, :] = y_ref[at, :] + y if first else y
+                    y_ref[at, :] = (y_ref[at, :] if first else skip * u) + y
                 return tuple(hs), tuple(ms)
 
             lax.fori_loop(0, tokens // BLOCK, step, ((zero,) * span, (zero,) * span))
@@ -233,26 +236,25 @@
                 t = n * BLOCK + i
                 at = tile(t if forward else tokens - 1 - t, tiles, h)
                 parts = [x * aged_ref[n, row : row + HALF, :] for x, row in zip(taps, rows)]
-                y_ref[at, :] = y_ref[at, :] + tree_sum(parts)
+                y_ref[at, :] = tree_sum(parts)
             return 0
 
-        lax.fori_loop(0, BLOCK, step, 0)
+        lax.fori_loop(0, BLOCK, step, 0, unroll=2)
 
 
 def mix_kernel(
-    dims, local_hbm, u_ref, gate_hbm, cot_hbm, skip_hbm, gain_hbm, a_ref, r_ref, in_ref, mixed_ref, sums_ref,
-    gate_ref, cot_ref, skip_ref, gain_ref, power_ref, taps_ref, aged_ref, y_ref, acc_ref, sem,
+    dims, local_hbm, gate_hbm, cot_hbm, gain_hbm, a_ref, r_ref, in_ref, mixed_ref, sums_ref,
+    local_ref, gate_ref, cot_ref, gain_ref, power_ref, taps_ref, aged_ref, y_ref, acc_ref, sem,
 ):
     tokens, tiles, modes, members, per = dims
     copies = fetch(
-        [(local_hbm, y_ref), (gate_hbm, gate_ref), (cot_hbm, cot_ref), (skip_hbm, skip_ref), (gain_hbm, gain_ref)], sem
+        [(local_hbm, local_ref), (gate_hbm, gate_ref), (cot_hbm, cot_ref), (gain_hbm, gain_ref)], sem
     )
     build_powers(r_ref, a_ref, taps_ref)
     block_power(a_ref, power_ref)
     age_states(dims, in_ref, power_ref, aged_ref)
-    copies[0].wait()
     add_arrived(dims, aged_ref, taps_ref, y_ref, True)
-    for copy in copies[1:]:
+    for copy in copies:
         copy.wait()
 
     def block(b, _):
@@ -262,7 +264,7 @@
         for j in range(tiles):
             cols = slice(j * LANES, (j + 1) * LANES)
             at = pl.ds(b * 16 * tiles + j, 16, stride=tiles)
-            mixed = y_ref[at, :] + skip_ref[:, cols] * u_ref[at, :]
+            mixed = y_ref[at, :] + local_ref[at, :]
             mixed_ref[rows, cols] = mixed
             premix = gate_ref[rows, cols].astype(F32) * mixed
             pull = cot_ref[rows, cols].astype(F32) * gain_ref[:, cols]
@@ -367,16 +369,20 @@
                 tuple(part_ref[0, row : row + HALF, :] for row in rows),
                 tuple(part_ref[1, row : row + HALF, :] for row in rows),
             )
-            lead, res, mom = lax.fori_loop(0, blocks, step, start)
+            lead, res, mom = lax.fori_loop(0, blocks, step, start, unroll=2)
             for i, row in enumerate(rows):
                 put_rows(send_ref, per, row, lead[i])
-                put_rows(send_ref, per, row, member_sums(res[i], mom[i], members), base=per)
+                for s, part in enumerate(member_sums(res[i], mom[i], members, per)):
+                    send_ref[row // per + s, per : per + 1, :] = part
         out += send_part(send_ref, send_hbm, out_sem, dims, first, span)
     for copy in save + out:
         copy.wait()
 
 
-def back_kernel(dims, row_ref, mixed_ref, gate_ref, cot_ref, gain_ref, w_ref, a_ref, r_ref, out_ref, grad_q_ref, y_ref):
+def back_kernel(
+    dims, row_ref, mixed_ref, gate_ref, cot_ref, gain_ref, w_ref, a_ref, r_ref, skip_ref, out_ref, grad_q_ref, y_hbm,
+    y_ref, sem,
+):
     tokens, tiles, modes, members, per = dims
 
     def block(b, _):
@@ -399,6 +405,7 @@
         rows = [i * tiles + h for i in range(modes)]
         a = [a_ref[row : row + HALF, :] for row in rows]
         res = [r_ref[row : row + HALF, :] for row in rows]
+        skip = skip_ref[h : h + HALF, :]
 
         def step(n, xs):
             for s in range(STEPS):
@@ -406,14 +413,19 @@
                 w = w_ref[at, :]
                 bs = [x + w for x in xs]
                 xs = [y * b for y, b in zip(a, bs)]
-                y_ref[at, :] = tree_sum([x * z for x, z in zip(res, bs)])
+                y_ref[at, :] = tree_sum([x * z for x, z in zip(res, bs)]) + skip * w
             return tuple(xs)
 
         lax.fori_loop(0, tokens // STEPS, step, (zero,) * modes)
-
-
-def suffix_kernel(dims, got_ref, both_ref, d_ref, after_hbm, send_ref):
-    tokens, tiles, modes, members, per = dims
+    for copy in fetch([(y_ref, y_hbm)], sem):
+        copy.wait()
+
+
+def suffix_kernel(dims, got_hbm, both_hbm, d_ref, after_hbm, send_ref, got_ref, both_ref, sem):
+    tokens, tiles, modes, members, per = dims
+    copies = fetch([(got_hbm, got_ref), (both_hbm, both_ref)], sem)
+    for copy in copies:
+        copy.wait()
     count = got_ref.shape[0]
     decay = d_ref[lax.axis_index("ctx")]
     zero = jnp.zeros((per, LANES), F32)
@@ -429,11 +441,11 @@
         mom = mom + lead * moment + float(tokens) * aged * before
         return aged + lead, part, mom
 
-    _, part, mom = lax.fori_loop(0, count, step, (zero,) * 3, unroll=8)
+    _, part, mom = lax.fori_loop(0, count, step, (zero, zero[:1], zero), unroll=8)
     pad = max(HALF - per, 0)
     if pad:
         mom = jnp.concatenate([mom, jnp.zeros((pad, LANES), F32)], axis=0)
-    part = part + member_sums(jnp.zeros_like(mom), mom, members)[:per]
+    part = part + member_sums(jnp.zeros_like(mom), mom, members, per)[0]
 
     def spread(i, _):
         send_ref[i, per:, :] = part
@@ -443,14 +455,14 @@
 
 
 def grad_kernel(
-    dims, total_tokens, got_ref, local_hbm, w_ref, k_hbm, v_hbm, skip_hbm, a_ref, r_ref, residue_hbm, log_hbm,
+    dims, total_tokens, got_ref, local_hbm, k_hbm, v_hbm, a_ref, r_ref, residue_hbm, log_hbm,
     grad_k_ref, grad_v_ref, grad_res_ref, grad_log_ref,
-    k_ref, v_ref, skip_ref, residue_ref, log_ref, power_ref, taps_ref, aged_ref, y_ref, tot_ref, sem,
+    local_ref, k_ref, v_ref, residue_ref, log_ref, power_ref, taps_ref, aged_ref, y_ref, tot_ref, sem,
 ):
     tokens, tiles, modes, members, per = dims
     copies = fetch(
         [
-            (local_hbm, y_ref), (k_hbm, k_ref), (v_hbm, v_ref), (skip_hbm, skip_ref),
+            (local_hbm, local_ref), (k_hbm, k_ref), (v_hbm, v_ref),
             (residue_hbm, residue_ref), (log_hbm, log_ref),
         ],
         sem,
@@ -458,9 +470,8 @@
     build_powers(r_ref, a_ref, taps_ref)
     block_power(a_ref, power_ref)
     age_states(dims, got_ref, power_ref, aged_ref)
-    copies[0].wait()
     add_arrived(dims, aged_ref, taps_ref, y_ref, False)
-    for copy in copies[1:]:
+    for copy in copies:
         copy.wait()
 
     def block(b, _):
@@ -468,23 +479,24 @@
         for j in range(tiles):
             cols = slice(j * LANES, (j + 1) * LANES)
             at = pl.ds(b * 16 * tiles + j, 16, stride=tiles)
-            grad = y_ref[at, :] + skip_ref[:, cols] * w_ref[at, :]
+            grad = y_ref[at, :] + local_ref[at, :]
             grad_k_ref[rows, cols] = (grad * v_ref[rows, cols].astype(F32)).astype(jnp.bfloat16)
             grad_v_ref[rows, cols] = (grad * k_ref[rows, cols].astype(F32)).astype(jnp.bfloat16)
         return 0
 
     lax.fori_loop(0, tokens // 16, block, 0)
 
-    for row in range(0, modes * tiles, HALF):
-        tot_ref[row : row + HALF, :] = get_rows(got_ref, per, row, base=per)
+    for piece in range(modes * tiles // per):
+        tot_ref[piece : piece + 1, :] = got_ref[piece, per : per + 1, :]
     groups = LANES // members
     lane = iota((modes, LANES), 1)
     first = second = jnp.zeros((modes, LANES), F32)
     for j in range(tiles):
-        value = tot_ref[pl.ds(j, modes, stride=tiles), :]
+        value = tot_ref[pl.ds(j // per, modes, stride=tiles // per), :]
+        at = 2 * groups * (j % per) + lane % groups
         own = lane // groups == j
-        first = jnp.where(own, jnp.take_along_axis(value, lane % groups, axis=1), first)
-        second = jnp.where(own, jnp.take_along_axis(value, groups + lane % groups, axis=1), second)
+        first = jnp.where(own, jnp.take_along_axis(value, at, axis=1), first)
+        second = jnp.where(own, jnp.take_along_axis(value, groups + at, axis=1), second)
     grad_res_ref[...] = first / total_tokens
     grad_log_ref[...] = -residue_ref[...] * jnp.exp(log_ref[...]) * second / total_tokens
 
@@ -520,10 +532,12 @@
     flat, state = ((tokens * tiles, LANES), F32), ((states, LANES), F32)
     powers, starts = ((BLOCK + 1, states, LANES), F32), ((blocks, states, LANES), F32)
     one, two = ((shards, per, LANES), F32), ((shards, 2 * per, LANES), F32)
+    one_rows = ((shards, LANES), F32)
+    wide = ((shards, per + 1, LANES), F32)
     narrow, small = ((tokens, channels), bf16), ((modes, groups), F32)
     rows = ((2, tokens, LANES), F32)
     line = ((1, channels), F32)
-    skip, gain = skip[None], gain[None]
+    skip, gain = skip.reshape(tiles, LANES), gain[None]
     residue, log_decay = residue.T, log_decay.T
 
     def exchange(value):
@@ -547,37 +561,37 @@
         [state, flat, flat, starts, starts],
         [flat, starts, starts, sems(4)],
         out_hbm=(1, 2, 3, 4),
-    )(u, a, residue)
+    )(u, a, residue, skip)
     both, send = call(functools.partial(prefix_kernel, per), "prefix", [two, one], hbm=(2,))(got, d, start)
     before = exchange(send)
     mixed, sums = call(
         functools.partial(mix_kernel, dims),
         "mix",
         [((tokens, channels), F32), ((2, tokens), F32)],
-        [narrow, narrow, line, line, state, powers, starts, flat, rows, sems(5)],
-        hbm=(0, 2, 3, 4, 5),
-    )(local, u, out_gate, cotangent, skip, gain, a, r, before)
+        [flat, narrow, narrow, line, state, powers, starts, flat, rows, sems(4)],
+        hbm=(0, 1, 2, 3),
+    )(local, out_gate, cotangent, gain, a, r, before)
     sums = lax.all_gather(sums, "tp")
     w, send, row = call(
         functools.partial(norm_kernel, dims, width),
         "norm",
-        [flat, two, rows],
-        [rows, two, flat, starts, starts, powers, starts, ((2, states, LANES), F32), sems(3), sems(3)],
+        [flat, wide, rows],
+        [rows, wide, flat, starts, starts, powers, starts, ((2, states, LANES), F32), sems(3), sems(3)],
         hbm=(7, 8, 9),
         out_hbm=(1, 2),
     )(sums, mixed, out_gate, cotangent, gain, a, before, far_u, start, moment)
     got = exchange(send)
-    mixer_out, grad_q, local = call(functools.partial(back_kernel, dims), "back", [narrow, narrow, flat])(
-        row, mixed, out_gate, cotangent, gain, w, a, r
+    mixer_out, grad_q, local = call(functools.partial(back_kernel, dims), "back", [narrow, narrow, flat], [flat, sems(1)], out_hbm=(2,))(
+        row, mixed, out_gate, cotangent, gain, w, a, r, skip
     )
-    (send,) = call(functools.partial(suffix_kernel, dims), "suffix", [two], hbm=(3,))(got, both, d, grad_q)
+    (send,) = call(functools.partial(suffix_kernel, dims), "suffix", [wide], [wide, two, sems(2)], hbm=(0, 1, 3))(got, both, d, grad_q)
     grad_k, grad_v, grad_residue, grad_log_decay = call(
         functools.partial(grad_kernel, dims, float(tokens * shards)),
         "grad",
         [narrow, narrow, small, small],
-        [narrow, narrow, line, small, small, state, powers, starts, flat, state, sems(6)],
-        hbm=(1, 3, 4, 5, 8, 9),
-    )(exchange(send), local, w, key_proj, value_proj, skip, a, r, residue, log_decay)
+        [flat, narrow, narrow, small, small, state, powers, starts, flat, one_rows, sems(5)],
+        hbm=(1, 2, 3, 6, 7),
+    )(exchange(send), local, key_proj, value_proj, a, r, residue, log_decay)
     return (mixer_out, grad_q, grad_k, grad_v, grad_residue.T, grad_log_decay.T)
 
 

time: 109 us -> 106 us (0.972)
  local copies, waits for them, and re-layouts: 2.85 us -> 0.93 us
  Pallas kernels: 29.8 us -> 28.5 us
    unnamed x16 -> x14, local copies, waits for them, and re-layouts: 2.85 us -> 0.93 us
    pallas_call x8, Pallas kernels: 29.8 us -> 28.5 us  [call(): pl.pallas_call(kernel, name=name, out_shape=[pltpu.HBM(s, d) if i in out_...]
  transfers between devices with their start and end apart: 2 -> 2, of which waited for: 2 -> 2; matrix products, arithmetic and copies ran while one was open for 0% -> 0% of each run, Pallas kernels for 8% -> 10%
where the time goes in v3:
time: 106 us; the launch traced here: 105 us
  blocking collectives  42 us (40%)
  Pallas kernels  28.5 us (27%)
  starting transfers between devices  20.2 us (19%)
  waiting for transfers between devices  12.8 us (12%)
    all_to_all x2, blocking collectives, exchange(): return lax.all_to_all(value, 'ctx', 0, 0, tiled=True)  34 us
    pallas_call x8, Pallas kernels, call(): pl.pallas_call(kernel, name=name, out_shape=[pltpu.HBM(s, d) if i in out_...  28.5 us
    all_to_all x2, starting transfers between devices, exchange(): return lax.all_to_all(value, 'ctx', 0, 0, tiled=True)  20.2 us
    all_to_all x2, waiting for transfers between devices, exchange(): return lax.all_to_all(value, 'ctx', 0, 0, tiled=True)  12.8 us
    all_gather x1, blocking collectives, per_device(): sums = lax.all_gather(sums, 'tp')  7.97 us
  transfers between devices with their start and end apart: 2, of which 2 were waited for; matrix products, arithmetic and copies ran while one was open for 0% of the time, Pallas kernels for 10%

profile of v3, /device:TPU:1, one launch (start us, length us, event | category | flops | bytes accessed | tf_op | source)
XLA Modules:
  0.0 105.3 jit_solution(11465260445017233225)
XLA Ops:
  0.6 4.2 %state.1 = (f32[2048,128]{1,0:T(8,128)S(1)}, f32[256,128]{1,0:T(8,128)S(1)}, f32[64,4,128]{2,1,0:T(4,128)S(1)}, f32[64,8,128]{2,1,0:T(8,128)}) custom-call(bf16[128,2048]{1,0:T(8,128)(2,1)} %k_hbm.3, bf16[128,2048]{1,0:T(8,128)(2,1)} %v_hbm.3, f32[16,128]{1,0:T(8,128)} %bitcast.15), custom_call_target="tpu_custom_call" | custom-call | tf_op jit(solution)/shard_map/state/pallas_call | solution.py:510
  4.9 0.0 copy-start.5
  4.9 0.0 copy-start.6
  4.9 13.0 %all-to-all-start = ((f32[64,8,128]{2,1,0:T(8,128)}), f32[64,8,128]{2,1,0:T(8,128)S(1)}, u32[]{:S(2)}, u32[]{:S(2)}) async-start(f32[64,8,128]{2,1,0:T(8,128)} %get-tuple-element.33), calls=%async_computation | async-start | bytes 524288 | tf_op jit(solution)/shard_map/all_to_all | solution.py:544
  17.9 0.0 copy-done.5
  17.9 0.0 copy-done.6
  17.9 5.3 %local.1 = (f32[256,128]{1,0:T(8,128)S(1)}, f32[2048,128]{1,0:T(8,128)}, f32[2048,128]{1,0:T(8,128)}, f32[8,256,128]{2,1,0:T(8,128)}, f32[8,256,128]{2,1,0:T(8,128)}) custom-call(f32[2048,128]{1,0:T(8,128)S(1)} %get-tuple-element.29.u_ref, f32[256,128]{1,0:T(8,128)S(1)} %get-tuple-element.30.a_ref, f32[16,128]{1,0:T(8,128)S(1)} %bitcast.13, ...), custom_call_target="tpu_custom_call" | custom-call | tf_op jit(solution)/shard_map/local/pallas_call | solution.py:510
  23.2 6.7 %all-to-all-done.got_ref = f32[64,8,128]{2,1,0:T(8,128)S(1)} async-done(((f32[64,8,128]{2,1,0:T(8,128)}), f32[64,8,128]{2,1,0:T(8,128)S(1)}, u32[]{:S(2)}, u32[]{:S(2)}) %all-to-all-start) | async-done | bytes 262176 | tf_op jit(solution)/shard_map/all_to_all | solution.py:544
  29.9 0.1 prefix.1
  30.0 16.2 %all_to_all.20.in_ref = f32[64,4,128]{2,1,0:T(4,128)S(1)} all-to-all(f32[64,4,128]{2,1,0:T(4,128)S(1)} %get-tuple-element.36), channel_id=1, replica_groups=mesh['ctx'=64,'tp'=4] {'ctx'}, dimensions={0} | all-to-all | bytes 262144 | tf_op jit(solution)/shard_map/all_to_all | solution.py:544
  46.2 2.5 %mix.1 = (f32[128,2048]{1,0:T(8,128)S(1)}, f32[2,128]{1,0:T(2,128)S(1)}) custom-call(f32[2048,128]{1,0:T(8,128)} %get-tuple-element.31.local_hbm, bf16[128,2048]{1,0:T(8,128)(2,1)} %gate_ref.3, bf16[128,2048]{1,0:T(8,128)(2,1)} %cot_ref.3, f32[1,2048]{1,0:T(1,128)} %bitcast.7, f32[256,128]{1,0:T(8,128)S(1)} %get-tuple-element.30.a_ref, ...), custom_call_target="tpu_custom_call" | custom-call | tf_op jit(solution)/shard_map/mix/pallas_call | solution.py:510
  48.7 0.0 copy-done.2
  48.7 0.0 copy-start.4
  48.7 8.0 %all-gather.1.sums_ref = f32[4,2,128]{2,1,0:T(2,128)S(1)} all-gather(f32[1,2,128]{2,1,0:T(2,128)S(1)} %bitcast.14), channel_id=2, replica_groups=mesh['ctx'=64,'tp'=4] {'tp'}, dimensions={0}, use_global_device_ids=true | all-gather | bytes 5120 | tf_op jit(solution)/shard_map/all_gather | solution.py:574
  56.7 0.0 copy-done.1
  56.7 6.5 %norm.1 = (f32[2048,128]{1,0:T(8,128)S(1)}, f32[64,5,128]{2,1,0:T(8,128)}, f32[2,128,128]{2,1,0:T(8,128)}) custom-call(f32[4,2,128]{2,1,0:T(2,128)S(1)} %all-gather.1.sums_ref, f32[128,2048]{1,0:T(8,128)S(1)} %get-tuple-element.38.mixed_ref, bf16[128,2048]{1,0:T(8,128)(2,1)S(1)} %copy-done, bf16[128,2048]{1,0:T(8,128)(2,1)S(1)} %copy-done.1, ...), custom_call_target="tpu_custom_call" | custom-call | tf_op jit(solution)/shard_map/norm/pallas_call | solution.py:510
  63.2 7.3 %all-to-all-start.2 = ((f32[64,5,128]{2,1,0:T(8,128)}), f32[64,5,128]{2,1,0:T(8,128)}, u32[]{:S(2)}, u32[]{:S(2)}) async-start(f32[64,5,128]{2,1,0:T(8,128)} %get-tuple-element.45), calls=%async_computation.2 | async-start | bytes 524288 | tf_op jit(solution)/shard_map/all_to_all | solution.py:544
  70.5 0.0 copy-start.3
  70.5 0.9 copy-done.3
  71.4 4.9 %back.1 = (bf16[128,2048]{1,0:T(8,128)(2,1)}, bf16[128,2048]{1,0:T(8,128)(2,1)}, f32[2048,128]{1,0:T(8,128)}) custom-call(f32[2,128,128]{2,1,0:T(8,128)S(1)} %copy-done.3, f32[128,2048]{1,0:T(8,128)S(1)} %get-tuple-element.38.mixed_ref, bf16[128,2048]{1,0:T(8,128)(2,1)S(1)} %copy-done, bf16[128,2048]{1,0:T(8,128)(2,1)S(1)} %copy-done.1, ...), custom_call_target="tpu_custom_call" | custom-call | tf_op jit(solution)/shard_map/back/pallas_call | solution.py:510
  76.3 6.1 %all-to-all-done.2.got_hbm = f32[64,5,128]{2,1,0:T(8,128)} async-done(((f32[64,5,128]{2,1,0:T(8,128)}), f32[64,5,128]{2,1,0:T(8,128)}, u32[]{:S(2)}, u32[]{:S(2)}) %all-to-all-start.2) | async-done | bytes 163872 | tf_op jit(solution)/shard_map/all_to_all | solution.py:544
  82.4 1.6 %suffix.1 = f32[64,5,128]{2,1,0:T(8,128)S(1)} custom-call(f32[64,5,128]{2,1,0:T(8,128)} %all-to-all-done.2.got_hbm, f32[64,8,128]{2,1,0:T(8,128)} %copy-done.2, f32[64,4,128]{2,1,0:T(4,128)S(1)} %get-tuple-element.34.d_ref, bf16[128,2048]{1,0:T(8,128)(2,1)} %get-tuple-element.24.after_hbm), custom_call_target="tpu_custom_call" | custom-call | tf_op jit(solution)/shard_map/suffix/pallas_call | solution.py:510
  84.0 17.9 %all_to_all.21.got_ref = f32[64,5,128]{2,1,0:T(8,128)S(1)} all-to-all(f32[64,5,128]{2,1,0:T(8,128)S(1)} %suffix.1), channel_id=1, replica_groups=mesh['ctx'=64,'tp'=4] {'ctx'}, dimensions={0} | all-to-all | bytes 327680 | tf_op jit(solution)/shard_map/all_to_all | solution.py:544
  101.9 3.4 %grad.1 = (bf16[128,2048]{1,0:T(8,128)(2,1)}, bf16[128,2048]{1,0:T(8,128)(2,1)}, f32[16,128]{1,0:T(8,128)}, f32[16,128]{1,0:T(8,128)}) custom-call(f32[64,5,128]{2,1,0:T(8,128)S(1)} %all_to_all.21.got_ref, f32[2048,128]{1,0:T(8,128)} %get-tuple-element.47.local_hbm, bf16[128,2048]{1,0:T(8,128)(2,1)} %k_hbm.3, bf16[128,2048]{1,0:T(8,128)(2,1)} %v_hbm.3, ...), custom_call_target="tpu_custom_call" | custom-call | tf_op jit(solution)/shard_map/grad/pallas_call | solution.py:510
  (5 shorter events, 0.0 us)
Async XLA Ops:
  4.9 13.0 %copy-start.5 = (f32[2048]{0:T(1024)S(1)}, f32[2048]{0:T(1024)}, u32[]{:S(2)}) copy-start(f32[2048]{0:T(1024)} %param.13) | copy-start | bytes 24580
  4.9 13.0 %copy-start.6 = (f32[128,16]{0,1:T(8,128)S(1)}, f32[128,16]{0,1:T(8,128)}, u32[]{:S(2)}) copy-start(f32[128,16]{0,1:T(8,128)} %param.11) | copy-start | bytes 24580
  4.9 25.0 %all-to-all-start = ((f32[64,8,128]{2,1,0:T(8,128)}), f32[64,8,128]{2,1,0:T(8,128)S(1)}, u32[]{:S(2)}, u32[]{:S(2)}) async-start(f32[64,8,128]{2,1,0:T(8,128)} %get-tuple-element.33), calls=%async_computation | async-start | bytes 524288 | tf_op jit(solution)/shard_map/all_to_all | solution.py:544
  30.0 18.7 %copy-start.2 = (f32[64,8,128]{2,1,0:T(8,128)}, f32[64,8,128]{2,1,0:T(8,128)S(1)}, u32[]{:S(2)}) copy-start(f32[64,8,128]{2,1,0:T(8,128)S(1)} %get-tuple-element.46.both_hbm) | copy-start | bytes 786436
  46.2 10.5 %copy-start = (bf16[128,2048]{1,0:T(8,128)(2,1)S(1)}, bf16[128,2048]{1,0:T(8,128)(2,1)}, u32[]{:S(2)}) copy-start(bf16[128,2048]{1,0:T(8,128)(2,1)} %gate_ref.3) | copy-start | bytes 1572868
  46.2 10.5 %copy-start.1 = (bf16[128,2048]{1,0:T(8,128)(2,1)S(1)}, bf16[128,2048]{1,0:T(8,128)(2,1)}, u32[]{:S(2)}) copy-start(bf16[128,2048]{1,0:T(8,128)(2,1)} %cot_ref.3) | copy-start | bytes 1572868
  48.7 8.0 %copy-start.4 = (f32[2048]{0:T(1024)S(1)}, f32[2048]{0:T(1024)}, u32[]{:S(2)}) copy-start(f32[2048]{0:T(1024)} %param.14) | copy-start | bytes 24580
  63.2 19.2 %all-to-all-start.2 = ((f32[64,5,128]{2,1,0:T(8,128)}), f32[64,5,128]{2,1,0:T(8,128)}, u32[]{:S(2)}, u32[]{:S(2)}) async-start(f32[64,5,128]{2,1,0:T(8,128)} %get-tuple-element.45), calls=%async_computation.2 | async-start | bytes 524288 | tf_op jit(solution)/shard_map/all_to_all | solution.py:544
  70.5 0.9 copy-start.3

commit v4 on v3

--- a/solution.py
+++ b/solution.py
@@ -20,18 +20,21 @@
 
 
 def get_rows(ref, per, row, base=0):
-    if per >= HALF:
-        return ref[row // per, base + row % per : base + row % per + HALF, :]
-    parts = [ref[row // per + s, base : base + per, :] for s in range(HALF // per)]
+    pieces = range(row // per, (row + HALF) // per)
+    if len(ref.shape) == 2:
+        parts = [ref[p * (per + 1) : p * (per + 1) + per, :] for p in pieces]
+    else:
+        parts = [ref[p, base : base + per, :] for p in pieces]
     return jnp.concatenate(parts, axis=0)
 
 
 def put_rows(ref, per, row, block, base=0):
-    if per >= HALF:
-        ref[row // per, base + row % per : base + row % per + HALF, :] = block
-    else:
-        for s in range(HALF // per):
-            ref[row // per + s, base : base + per, :] = block[s * per : (s + 1) * per]
+    for s in range(HALF // per):
+        p, part = row // per + s, block[s * per : (s + 1) * per]
+        if len(ref.shape) == 2:
+            ref[p * (per + 1) : p * (per + 1) + per, :] = part
+        else:
+            ref[p, base : base + per, :] = part
 
 
 def member_sums(first, second, members, per):
@@ -96,7 +99,8 @@
 
 def send_part(send_ref, send_hbm, sem, dims, first, span):
     tokens, tiles, modes, members, per = dims
-    pieces = pl.ds(first * tiles // per, span * tiles // per)
+    size = per + 1 if len(send_ref.shape) == 2 else 1
+    pieces = pl.ds(first * tiles // per * size, span * tiles // per * size)
     return fetch([(send_ref.at[pieces], send_hbm.at[pieces])], sem, first // span)
 
 
@@ -373,7 +377,8 @@
             for i, row in enumerate(rows):
                 put_rows(send_ref, per, row, lead[i])
                 for s, part in enumerate(member_sums(res[i], mom[i], members, per)):
-                    send_ref[row // per + s, per : per + 1, :] = part
+                    last = (row // per + s) * (per + 1) + per
+                    send_ref[last : last + 1, :] = part
         out += send_part(send_ref, send_hbm, out_sem, dims, first, span)
     for copy in save + out:
         copy.wait()
@@ -426,38 +431,32 @@
     copies = fetch([(got_hbm, got_ref), (both_hbm, both_ref)], sem)
     for copy in copies:
         copy.wait()
-    count = got_ref.shape[0]
+    count = both_ref.shape[0]
     decay = d_ref[lax.axis_index("ctx")]
-    zero = jnp.zeros((per, LANES), F32)
-
-    def step(n, carry):
-        after, part, mom = carry
-        i = count - 1 - n
-        got, both = got_ref[i], both_ref[i]
-        lead, before, moment = got[:per], both[:per], both[per:]
-        send_ref[i, :per, :] = after
+    after = mom = jnp.zeros((per, LANES), F32)
+    part = jnp.zeros((1, LANES), F32)
+    for i in range(count - 1, -1, -1):
+        row = i * (per + 1)
+        lead, both = got_ref[row : row + per, :], both_ref[i]
+        before, moment = both[:per], both[per:]
+        send_ref[row : row + per, :] = after
         aged = decay * after
-        part = part + got[per:]
+        part = part + got_ref[row + per : row + per + 1, :]
         mom = mom + lead * moment + float(tokens) * aged * before
-        return aged + lead, part, mom
-
-    _, part, mom = lax.fori_loop(0, count, step, (zero, zero[:1], zero), unroll=8)
+        after = aged + lead
     pad = max(HALF - per, 0)
     if pad:
         mom = jnp.concatenate([mom, jnp.zeros((pad, LANES), F32)], axis=0)
     part = part + member_sums(jnp.zeros_like(mom), mom, members, per)[0]
-
-    def spread(i, _):
-        send_ref[i, per:, :] = part
-        return 0
-
-    lax.fori_loop(0, count, spread, 0, unroll=8)
+    for i in range(count):
+        row = i * (per + 1) + per
+        send_ref[row : row + 1, :] = part
 
 
 def grad_kernel(
     dims, total_tokens, got_ref, local_hbm, k_hbm, v_hbm, a_ref, r_ref, residue_hbm, log_hbm,
     grad_k_ref, grad_v_ref, grad_res_ref, grad_log_ref,
-    local_ref, k_ref, v_ref, residue_ref, log_ref, power_ref, taps_ref, aged_ref, y_ref, tot_ref, sem,
+    local_ref, k_ref, v_ref, residue_ref, log_ref, power_ref, taps_ref, aged_ref, y_ref, sem,
 ):
     tokens, tiles, modes, members, per = dims
     copies = fetch(
@@ -486,13 +485,12 @@
 
     lax.fori_loop(0, tokens // 16, block, 0)
 
-    for piece in range(modes * tiles // per):
-        tot_ref[piece : piece + 1, :] = got_ref[piece, per : per + 1, :]
     groups = LANES // members
     lane = iota((modes, LANES), 1)
     first = second = jnp.zeros((modes, LANES), F32)
     for j in range(tiles):
-        value = tot_ref[pl.ds(j // per, modes, stride=tiles // per), :]
+        size = per + 1
+        value = got_ref[pl.ds(j // per * size + per, modes, stride=tiles // per * size), :]
         at = 2 * groups * (j % per) + lane % groups
         own = lane // groups == j
         first = jnp.where(own, jnp.take_along_axis(value, at, axis=1), first)
@@ -532,8 +530,7 @@
     flat, state = ((tokens * tiles, LANES), F32), ((states, LANES), F32)
     powers, starts = ((BLOCK + 1, states, LANES), F32), ((blocks, states, LANES), F32)
     one, two = ((shards, per, LANES), F32), ((shards, 2 * per, LANES), F32)
-    one_rows = ((shards, LANES), F32)
-    wide = ((shards, per + 1, LANES), F32)
+    wide = ((shards * (per + 1), LANES), F32)
     narrow, small = ((tokens, channels), bf16), ((modes, groups), F32)
     rows = ((2, tokens, LANES), F32)
     line = ((1, channels), F32)
@@ -541,7 +538,10 @@
     residue, log_decay = residue.T, log_decay.T
 
     def exchange(value):
-        return lax.all_to_all(value, "ctx", 0, 0, tiled=True)
+        shape = value.shape
+        if len(shape) == 2:
+            value = value.reshape(shards, 1, -1)
+        return lax.all_to_all(value, "ctx", 0, 0, tiled=True).reshape(shape)
 
     def sems(n):
         return pltpu.SemaphoreType.DMA((n,))
@@ -589,7 +589,7 @@
         functools.partial(grad_kernel, dims, float(tokens * shards)),
         "grad",
         [narrow, narrow, small, small],
-        [flat, narrow, narrow, small, small, state, powers, starts, flat, one_rows, sems(5)],
+        [flat, narrow, narrow, small, small, state, powers, starts, flat, sems(5)],
         hbm=(1, 2, 3, 6, 7),
     )(exchange(send), local, key_proj, value_proj, a, r, residue, log_decay)
     return (mixer_out, grad_q, grad_k, grad_v, grad_residue.T, grad_log_decay.T)

time: 106 us -> 102 us (0.962)
  blocking collectives: 42 us -> 40.1 us
  waiting for transfers between devices: 12.8 us -> 11.5 us
    all_to_all x2, blocking collectives: 34 us -> 32.2 us  [exchange(): return lax.all_to_all(value, 'ctx', 0, 0, tiled=True).reshape(shape)]
    all_to_all x2, waiting for transfers between devices: 12.8 us -> 11.5 us  [exchange(): return lax.all_to_all(value, 'ctx', 0, 0, tiled=True).reshape(shape)]
where the time goes in v4:
time: 102 us
  blocking collectives  40.1 us (39%)
  Pallas kernels  28.5 us (28%)
  starting transfers between devices  20.2 us (20%)
  waiting for transfers between devices  11.5 us (11%)
    all_to_all x2, blocking collectives, exchange(): return lax.all_to_all(value, 'ctx', 0, 0, tiled=True).reshape(shape)  32.2 us
    pallas_call x8, Pallas kernels, call(): pl.pallas_call(kernel, name=name, out_shape=[pltpu.HBM(s, d) if i in out_...  28.5 us
    all_to_all x2, starting transfers between devices, exchange(): return lax.all_to_all(value, 'ctx', 0, 0, tiled=True).reshape(shape)  20.2 us
    all_to_all x2, waiting for transfers between devices, exchange(): return lax.all_to_all(value, 'ctx', 0, 0, tiled=True).reshape(shape)  11.5 us
    all_gather x1, blocking collectives, per_device(): sums = lax.all_gather(sums, 'tp')  7.97 us
  transfers between devices with their start and end apart: 2, of which 2 were waited for; matrix products, arithmetic and copies ran while one was open for 0% of the time, Pallas kernels for 10%

profile of v4, /device:TPU:1, one launch (start us, length us, event | category | flops | bytes accessed | tf_op | source)
XLA Modules:
  0.0 102.0 jit_solution(17808127931116058398)
XLA Ops:
  0.6 4.2 %state.1 = (f32[2048,128]{1,0:T(8,128)S(1)}, f32[256,128]{1,0:T(8,128)S(1)}, f32[64,4,128]{2,1,0:T(4,128)S(1)}, f32[64,8,128]{2,1,0:T(8,128)}) custom-call(bf16[128,2048]{1,0:T(8,128)(2,1)} %k_hbm.3, bf16[128,2048]{1,0:T(8,128)(2,1)} %v_hbm.3, f32[16,128]{1,0:T(8,128)} %bitcast.22), custom_call_target="tpu_custom_call" | custom-call | tf_op jit(solution)/shard_map/state/pallas_call | solution.py:508
  4.9 0.0 copy-start.5
  4.9 0.0 copy-start.6
  4.9 13.0 %all-to-all-start = ((f32[64,8,128]{2,1,0:T(8,128)}), f32[64,8,128]{2,1,0:T(8,128)S(1)}, u32[]{:S(2)}, u32[]{:S(2)}) async-start(f32[64,8,128]{2,1,0:T(8,128)} %get-tuple-element.33), calls=%async_computation | async-start | bytes 524288 | tf_op jit(solution)/shard_map/all_to_all | solution.py:544
  17.9 0.0 copy-done.5
  17.9 0.0 copy-done.6
  17.9 5.3 %local.1 = (f32[256,128]{1,0:T(8,128)S(1)}, f32[2048,128]{1,0:T(8,128)}, f32[2048,128]{1,0:T(8,128)}, f32[8,256,128]{2,1,0:T(8,128)}, f32[8,256,128]{2,1,0:T(8,128)}) custom-call(f32[2048,128]{1,0:T(8,128)S(1)} %get-tuple-element.29.u_ref, f32[256,128]{1,0:T(8,128)S(1)} %get-tuple-element.30.a_ref, f32[16,128]{1,0:T(8,128)S(1)} %bitcast.19, ...), custom_call_target="tpu_custom_call" | custom-call | tf_op jit(solution)/shard_map/local/pallas_call | solution.py:508
  23.2 6.7 %all-to-all-done.got_ref = f32[64,8,128]{2,1,0:T(8,128)S(1)} async-done(((f32[64,8,128]{2,1,0:T(8,128)}), f32[64,8,128]{2,1,0:T(8,128)S(1)}, u32[]{:S(2)}, u32[]{:S(2)}) %all-to-all-start) | async-done | bytes 262176 | tf_op jit(solution)/shard_map/all_to_all | solution.py:544
  29.9 0.1 prefix.1
  30.0 16.2 %all_to_all.20.in_ref = f32[64,4,128]{2,1,0:T(4,128)S(1)} all-to-all(f32[64,4,128]{2,1,0:T(4,128)S(1)} %get-tuple-element.36), channel_id=1, replica_groups=mesh['ctx'=64,'tp'=4] {'ctx'}, dimensions={0} | all-to-all | bytes 262144 | tf_op jit(solution)/shard_map/all_to_all | solution.py:544
  46.2 2.5 %mix.1 = (f32[128,2048]{1,0:T(8,128)S(1)}, f32[2,128]{1,0:T(2,128)S(1)}) custom-call(f32[2048,128]{1,0:T(8,128)} %get-tuple-element.31.local_hbm, bf16[128,2048]{1,0:T(8,128)(2,1)} %gate_ref.3, bf16[128,2048]{1,0:T(8,128)(2,1)} %cot_ref.3, f32[1,2048]{1,0:T(1,128)} %bitcast.13, f32[256,128]{1,0:T(8,128)S(1)} %get-tuple-element.30.a_ref, ...), custom_call_target="tpu_custom_call" | custom-call | tf_op jit(solution)/shard_map/mix/pallas_call | solution.py:508
  48.7 0.0 copy-done.2
  48.7 0.0 copy-start.4
  48.7 8.0 %all-gather.1.sums_ref = f32[4,2,128]{2,1,0:T(2,128)S(1)} all-gather(f32[1,2,128]{2,1,0:T(2,128)S(1)} %bitcast.20), channel_id=2, replica_groups=mesh['ctx'=64,'tp'=4] {'tp'}, dimensions={0}, use_global_device_ids=true | all-gather | bytes 5120 | tf_op jit(solution)/shard_map/all_gather | solution.py:574
  56.7 0.0 copy-done.4
  56.7 6.5 %norm.1 = (f32[2048,128]{1,0:T(8,128)S(1)}, f32[320,128]{1,0:T(8,128)}, f32[2,128,128]{2,1,0:T(8,128)}) custom-call(f32[4,2,128]{2,1,0:T(2,128)S(1)} %all-gather.1.sums_ref, f32[128,2048]{1,0:T(8,128)S(1)} %get-tuple-element.38.mixed_ref, bf16[128,2048]{1,0:T(8,128)(2,1)S(1)} %copy-done, bf16[128,2048]{1,0:T(8,128)(2,1)S(1)} %copy-done.1, ...), custom_call_target="tpu_custom_call" | custom-call | tf_op jit(solution)/shard_map/norm/pallas_call | solution.py:508
  63.2 7.2 %all-to-all-start.2 = ((f32[64,1,640]{2,1,0:T(1,128)}), f32[64,1,640]{2,1,0:T(1,128)}, u32[]{:S(2)}, u32[]{:S(2)}) async-start(f32[64,1,640]{2,1,0:T(1,128)} %bitcast.21), calls=%async_computation.2 | async-start | bytes 327680 | tf_op jit(solution)/shard_map/all_to_all | solution.py:544
  70.4 0.0 copy-start.3
  70.5 0.9 copy-done.3
  71.4 4.9 %back.1 = (bf16[128,2048]{1,0:T(8,128)(2,1)}, bf16[128,2048]{1,0:T(8,128)(2,1)}, f32[2048,128]{1,0:T(8,128)}) custom-call(f32[2,128,128]{2,1,0:T(8,128)S(1)} %copy-done.3, f32[128,2048]{1,0:T(8,128)S(1)} %get-tuple-element.38.mixed_ref, bf16[128,2048]{1,0:T(8,128)(2,1)S(1)} %copy-done, bf16[128,2048]{1,0:T(8,128)(2,1)S(1)} %copy-done.1, ...), custom_call_target="tpu_custom_call" | custom-call | tf_op jit(solution)/shard_map/back/pallas_call | solution.py:508
  76.2 4.9 %all-to-all-done.2 = f32[64,1,640]{2,1,0:T(1,128)} async-done(((f32[64,1,640]{2,1,0:T(1,128)}), f32[64,1,640]{2,1,0:T(1,128)}, u32[]{:S(2)}, u32[]{:S(2)}) %all-to-all-start.2) | async-done | bytes 163872 | tf_op jit(solution)/shard_map/all_to_all | solution.py:544
  81.1 1.6 %suffix.1 = f32[320,128]{1,0:T(8,128)S(1)} custom-call(f32[320,128]{1,0:T(8,128)} %bitcast.6.got_hbm, f32[64,8,128]{2,1,0:T(8,128)} %copy-done.2, f32[64,4,128]{2,1,0:T(4,128)S(1)} %get-tuple-element.34.d_ref, bf16[128,2048]{1,0:T(8,128)(2,1)} %get-tuple-element.24.after_hbm), custom_call_target="tpu_custom_call" | custom-call | tf_op jit(solution)/shard_map/suffix/pallas_call | solution.py:508
  82.7 16.0 %all_to_all.21 = f32[64,1,640]{2,1,0:T(1,128)S(1)} all-to-all(f32[64,1,640]{2,1,0:T(1,128)S(1)} %bitcast.12), channel_id=1, replica_groups=mesh['ctx'=64,'tp'=4] {'ctx'}, dimensions={0} | all-to-all | bytes 327680 | tf_op jit(solution)/shard_map/all_to_all | solution.py:544
  98.7 3.4 %grad.1 = (bf16[128,2048]{1,0:T(8,128)(2,1)}, bf16[128,2048]{1,0:T(8,128)(2,1)}, f32[16,128]{1,0:T(8,128)}, f32[16,128]{1,0:T(8,128)}) custom-call(f32[320,128]{1,0:T(8,128)S(1)} %bitcast.11, f32[2048,128]{1,0:T(8,128)} %get-tuple-element.47.local_hbm, bf16[128,2048]{1,0:T(8,128)(2,1)} %k_hbm.3, bf16[128,2048]{1,0:T(8,128)(2,1)} %v_hbm.3, ...), custom_call_target="tpu_custom_call" | custom-call | tf_op jit(solution)/shard_map/grad/pallas_call | solution.py:508
  (5 shorter events, 0.0 us)
Async XLA Ops:
  4.9 13.0 %copy-start.5 = (f32[2048]{0:T(1024)S(1)}, f32[2048]{0:T(1024)}, u32[]{:S(2)}) copy-start(f32[2048]{0:T(1024)} %param.13) | copy-start | bytes 24580
  4.9 13.0 %copy-start.6 = (f32[128,16]{0,1:T(8,128)S(1)}, f32[128,16]{0,1:T(8,128)}, u32[]{:S(2)}) copy-start(f32[128,16]{0,1:T(8,128)} %param.11) | copy-start | bytes 24580
  4.9 25.0 %all-to-all-start = ((f32[64,8,128]{2,1,0:T(8,128)}), f32[64,8,128]{2,1,0:T(8,128)S(1)}, u32[]{:S(2)}, u32[]{:S(2)}) async-start(f32[64,8,128]{2,1,0:T(8,128)} %get-tuple-element.33), calls=%async_computation | async-start | bytes 524288 | tf_op jit(solution)/shard_map/all_to_all | solution.py:544
  30.0 18.7 %copy-start.2 = (f32[64,8,128]{2,1,0:T(8,128)}, f32[64,8,128]{2,1,0:T(8,128)S(1)}, u32[]{:S(2)}) copy-start(f32[64,8,128]{2,1,0:T(8,128)S(1)} %get-tuple-element.46.both_hbm) | copy-start | bytes 786436
  46.2 10.5 %copy-start = (bf16[128,2048]{1,0:T(8,128)(2,1)S(1)}, bf16[128,2048]{1,0:T(8,128)(2,1)}, u32[]{:S(2)}) copy-start(bf16[128,2048]{1,0:T(8,128)(2,1)} %gate_ref.3) | copy-start | bytes 1572868
  46.2 10.5 %copy-start.1 = (bf16[128,2048]{1,0:T(8,128)(2,1)S(1)}, bf16[128,2048]{1,0:T(8,128)(2,1)}, u32[]{:S(2)}) copy-start(bf16[128,2048]{1,0:T(8,128)(2,1)} %cot_ref.3) | copy-start | bytes 1572868
  48.7 8.0 %copy-start.4 = (f32[2048]{0:T(1024)S(1)}, f32[2048]{0:T(1024)}, u32[]{:S(2)}) copy-start(f32[2048]{0:T(1024)} %param.14) | copy-start | bytes 24580
  63.2 17.9 %all-to-all-start.2 = ((f32[64,1,640]{2,1,0:T(1,128)}), f32[64,1,640]{2,1,0:T(1,128)}, u32[]{:S(2)}, u32[]{:S(2)}) async-start(f32[64,1,640]{2,1,0:T(1,128)} %bitcast.21), calls=%async_computation.2 | async-start | bytes 327680 | tf_op jit(solution)/shard_map/all_to_all | solution.py:544
  70.4 0.9 copy-start.3

commit v5 on v4

--- a/solution.py
+++ b/solution.py
@@ -385,10 +385,13 @@
 
 
 def back_kernel(
-    dims, row_ref, mixed_ref, gate_ref, cot_ref, gain_ref, w_ref, a_ref, r_ref, skip_ref, out_ref, grad_q_ref, y_hbm,
-    y_ref, sem,
+    dims, row_hbm, mixed_ref, gate_hbm, cot_hbm, gain_ref, w_ref, a_ref, r_ref, skip_ref, both_hbm,
+    out_ref, grad_q_ref, y_hbm, both_ref, row_ref, gate_ref, cot_ref, y_ref, sem,
 ):
     tokens, tiles, modes, members, per = dims
+    pairs = [(row_hbm, row_ref), (gate_hbm, gate_ref), (cot_hbm, cot_ref), (both_hbm, both_ref)]
+    for copy in fetch(pairs, sem, 1):
+        copy.wait()
 
     def block(b, _):
         rows = pl.ds(pl.multiple_of(b * 16, 16), 16)
@@ -426,11 +429,8 @@
         copy.wait()
 
 
-def suffix_kernel(dims, got_hbm, both_hbm, d_ref, after_hbm, send_ref, got_ref, both_ref, sem):
-    tokens, tiles, modes, members, per = dims
-    copies = fetch([(got_hbm, got_ref), (both_hbm, both_ref)], sem)
-    for copy in copies:
-        copy.wait()
+def suffix_kernel(dims, got_ref, both_ref, d_ref, send_ref):
+    tokens, tiles, modes, members, per = dims
     count = both_ref.shape[0]
     decay = d_ref[lax.axis_index("ctx")]
     after = mom = jnp.zeros((per, LANES), F32)
@@ -455,8 +455,8 @@
 
 def grad_kernel(
     dims, total_tokens, got_ref, local_hbm, k_hbm, v_hbm, a_ref, r_ref, residue_hbm, log_hbm,
-    grad_k_ref, grad_v_ref, grad_res_ref, grad_log_ref,
-    local_ref, k_ref, v_ref, residue_ref, log_ref, power_ref, taps_ref, aged_ref, y_ref, sem,
+    grad_k_hbm, grad_v_hbm, grad_res_hbm, grad_log_hbm,
+    grad_k_ref, grad_v_ref, grad_res_ref, grad_log_ref, local_ref, k_ref, v_ref, residue_ref, log_ref, power_ref, taps_ref, aged_ref, y_ref, sem, out_sem,
 ):
     tokens, tiles, modes, members, per = dims
     copies = fetch(
@@ -472,19 +472,6 @@
     add_arrived(dims, aged_ref, taps_ref, y_ref, False)
     for copy in copies:
         copy.wait()
-
-    def block(b, _):
-        rows = pl.ds(pl.multiple_of(b * 16, 16), 16)
-        for j in range(tiles):
-            cols = slice(j * LANES, (j + 1) * LANES)
-            at = pl.ds(b * 16 * tiles + j, 16, stride=tiles)
-            grad = y_ref[at, :] + local_ref[at, :]
-            grad_k_ref[rows, cols] = (grad * v_ref[rows, cols].astype(F32)).astype(jnp.bfloat16)
-            grad_v_ref[rows, cols] = (grad * k_ref[rows, cols].astype(F32)).astype(jnp.bfloat16)
-        return 0
-
-    lax.fori_loop(0, tokens // 16, block, 0)
-
     groups = LANES // members
     lane = iota((modes, LANES), 1)
     first = second = jnp.zeros((modes, LANES), F32)
@@ -497,6 +484,32 @@
         second = jnp.where(own, jnp.take_along_axis(value, groups + at, axis=1), second)
     grad_res_ref[...] = first / total_tokens
     grad_log_ref[...] = -residue_ref[...] * jnp.exp(log_ref[...]) * second / total_tokens
+    copies = fetch([(grad_res_ref, grad_res_hbm), (grad_log_ref, grad_log_hbm)], out_sem)
+
+    def halves(b):
+        rows = pl.ds(pl.multiple_of(b * 16, 16), 16)
+        return [
+            pltpu.make_async_copy(grad_k_ref.at[rows, :], grad_k_hbm.at[rows, :], out_sem.at[2 + 2 * b]),
+            pltpu.make_async_copy(grad_v_ref.at[rows, :], grad_v_hbm.at[rows, :], out_sem.at[3 + 2 * b]),
+        ]
+
+    def block(b, _):
+        rows = pl.ds(pl.multiple_of(b * 16, 16), 16)
+        for j in range(tiles):
+            cols = slice(j * LANES, (j + 1) * LANES)
+            at = pl.ds(b * 16 * tiles + j, 16, stride=tiles)
+            grad = y_ref[at, :] + local_ref[at, :]
+            grad_k_ref[rows, cols] = (grad * v_ref[rows, cols].astype(F32)).astype(jnp.bfloat16)
+            grad_v_ref[rows, cols] = (grad * k_ref[rows, cols].astype(F32)).astype(jnp.bfloat16)
+        for copy in halves(b):
+            copy.start()
+        return 0
+
+    lax.fori_loop(0, tokens // 16, block, 0)
+    for b in range(tokens // 16):
+        copies += halves(b)
+    for copy in copies:
+        copy.wait()
 
 
 def call(kernel, name, outs, scratch=(), hbm=(), out_hbm=()):
@@ -581,16 +594,22 @@
         out_hbm=(1, 2),
     )(sums, mixed, out_gate, cotangent, gain, a, before, far_u, start, moment)
     got = exchange(send)
-    mixer_out, grad_q, local = call(functools.partial(back_kernel, dims), "back", [narrow, narrow, flat], [flat, sems(1)], out_hbm=(2,))(
-        row, mixed, out_gate, cotangent, gain, w, a, r, skip
-    )
-    (send,) = call(functools.partial(suffix_kernel, dims), "suffix", [wide], [wide, two, sems(2)], hbm=(0, 1, 3))(got, both, d, grad_q)
+    mixer_out, grad_q, local, both = call(
+        functools.partial(back_kernel, dims),
+        "back",
+        [narrow, narrow, flat, two],
+        [rows, narrow, narrow, flat, sems(5)],
+        hbm=(0, 2, 3, 9),
+        out_hbm=(2,),
+    )(row, mixed, out_gate, cotangent, gain, w, a, r, skip, both)
+    (send,) = call(functools.partial(suffix_kernel, dims), "suffix", [wide])(got, both, d)
     grad_k, grad_v, grad_residue, grad_log_decay = call(
         functools.partial(grad_kernel, dims, float(tokens * shards)),
         "grad",
         [narrow, narrow, small, small],
-        [flat, narrow, narrow, small, small, state, powers, starts, flat, sems(5)],
+        [narrow, narrow, small, small, flat, narrow, narrow, small, small, state, powers, starts, flat, sems(5), sems(2 + tokens // 8)],
         hbm=(1, 2, 3, 6, 7),
+        out_hbm=(0, 1, 2, 3),
     )(exchange(send), local, key_proj, value_proj, a, r, residue, log_decay)
     return (mixer_out, grad_q, grad_k, grad_v, grad_residue.T, grad_log_decay.T)
 

time: 102 us -> 102 us (level)
  transfers between devices with their start and end apart: 2 -> 2, of which waited for: 2 -> 2; matrix products, arithmetic and copies ran while one was open for 0% -> 0% of each run, Pallas kernels for 10% -> 11%
where the time goes in v5:
time: 102 us
  blocking collectives  40.5 us (40%)
  Pallas kernels  28.8 us (28%)
  starting transfers between devices  19.9 us (20%)
  waiting for transfers between devices  11 us (11%)
    all_to_all x2, blocking collectives, exchange(): return lax.all_to_all(value, 'ctx', 0, 0, tiled=True).reshape(shape)  32.5 us
    pallas_call x8, Pallas kernels, call(): pl.pallas_call(kernel, name=name, out_shape=[pltpu.HBM(s, d) if i in out_...  28.8 us
    all_to_all x2, starting transfers between devices, exchange(): return lax.all_to_all(value, 'ctx', 0, 0, tiled=True).reshape(shape)  19.9 us
    all_to_all x2, waiting for transfers between devices, exchange(): return lax.all_to_all(value, 'ctx', 0, 0, tiled=True).reshape(shape)  11 us
    all_gather x1, blocking collectives, per_device(): sums = lax.all_gather(sums, 'tp')  7.97 us
  transfers between devices with their start and end apart: 2, of which 2 were waited for; matrix products, arithmetic and copies ran while one was open for 0% of the time, Pallas kernels for 11%

profile of v5, /device:TPU:1, one launch (start us, length us, event | category | flops | bytes accessed | tf_op | source)
XLA Modules:
  0.0 101.8 jit_solution(11605749162545507243)
XLA Ops:
  0.6 4.2 %state.1 = (f32[2048,128]{1,0:T(8,128)S(1)}, f32[256,128]{1,0:T(8,128)S(1)}, f32[64,4,128]{2,1,0:T(4,128)S(1)}, f32[64,8,128]{2,1,0:T(8,128)}) custom-call(bf16[128,2048]{1,0:T(8,128)(2,1)} %k_hbm.3, bf16[128,2048]{1,0:T(8,128)(2,1)} %v_hbm.3, f32[16,128]{1,0:T(8,128)} %bitcast.23), custom_call_target="tpu_custom_call" | custom-call | tf_op jit(solution)/shard_map/state/pallas_call | solution.py:521
  4.9 0.0 copy-start.4
  4.9 0.0 copy-start.5
  4.9 13.0 %all-to-all-start = ((f32[64,8,128]{2,1,0:T(8,128)}), f32[64,8,128]{2,1,0:T(8,128)S(1)}, u32[]{:S(2)}, u32[]{:S(2)}) async-start(f32[64,8,128]{2,1,0:T(8,128)} %get-tuple-element.34), calls=%async_computation | async-start | bytes 524288 | tf_op jit(solution)/shard_map/all_to_all | solution.py:557
  17.9 0.0 copy-done.4
  17.9 0.0 copy-done.5
  17.9 5.3 %local.1 = (f32[256,128]{1,0:T(8,128)S(1)}, f32[2048,128]{1,0:T(8,128)}, f32[2048,128]{1,0:T(8,128)}, f32[8,256,128]{2,1,0:T(8,128)}, f32[8,256,128]{2,1,0:T(8,128)}) custom-call(f32[2048,128]{1,0:T(8,128)S(1)} %get-tuple-element.30.u_ref, f32[256,128]{1,0:T(8,128)S(1)} %get-tuple-element.31.a_ref, f32[16,128]{1,0:T(8,128)S(1)} %bitcast.20, ...), custom_call_target="tpu_custom_call" | custom-call | tf_op jit(solution)/shard_map/local/pallas_call | solution.py:521
  23.2 6.7 %all-to-all-done.got_ref = f32[64,8,128]{2,1,0:T(8,128)S(1)} async-done(((f32[64,8,128]{2,1,0:T(8,128)}), f32[64,8,128]{2,1,0:T(8,128)S(1)}, u32[]{:S(2)}, u32[]{:S(2)}) %all-to-all-start) | async-done | bytes 262176 | tf_op jit(solution)/shard_map/all_to_all | solution.py:557
  29.9 0.1 prefix.1
  30.0 0.7 copy-done.2
  30.7 16.2 %all_to_all.20.in_ref = f32[64,4,128]{2,1,0:T(4,128)S(1)} all-to-all(f32[64,4,128]{2,1,0:T(4,128)S(1)} %get-tuple-element.37), channel_id=1, replica_groups=mesh['ctx'=64,'tp'=4] {'ctx'}, dimensions={0} | all-to-all | bytes 262144 | tf_op jit(solution)/shard_map/all_to_all | solution.py:557
  46.9 2.5 %mix.1 = (f32[128,2048]{1,0:T(8,128)S(1)}, f32[2,128]{1,0:T(2,128)S(1)}) custom-call(f32[2048,128]{1,0:T(8,128)} %get-tuple-element.32.local_hbm, bf16[128,2048]{1,0:T(8,128)(2,1)} %gate_hbm.3, bf16[128,2048]{1,0:T(8,128)(2,1)} %cot_hbm.3, f32[1,2048]{1,0:T(1,128)} %bitcast.14, f32[256,128]{1,0:T(8,128)S(1)} %get-tuple-element.31.a_ref, ...), custom_call_target="tpu_custom_call" | custom-call | tf_op jit(solution)/shard_map/mix/pallas_call | solution.py:521
  49.4 0.0 copy-start.3
  49.4 8.0 %all-gather.1.sums_ref = f32[4,2,128]{2,1,0:T(2,128)S(1)} all-gather(f32[1,2,128]{2,1,0:T(2,128)S(1)} %bitcast.21), channel_id=2, replica_groups=mesh['ctx'=64,'tp'=4] {'tp'}, dimensions={0}, use_global_device_ids=true | all-gather | bytes 5120 | tf_op jit(solution)/shard_map/all_gather | solution.py:587
  57.4 0.0 copy-done
  57.4 0.0 copy-done.1
  57.4 0.0 copy-done.3
  57.4 6.5 %norm.1 = (f32[2048,128]{1,0:T(8,128)S(1)}, f32[320,128]{1,0:T(8,128)}, f32[2,128,128]{2,1,0:T(8,128)}) custom-call(f32[4,2,128]{2,1,0:T(2,128)S(1)} %all-gather.1.sums_ref, f32[128,2048]{1,0:T(8,128)S(1)} %get-tuple-element.39.mixed_ref, bf16[128,2048]{1,0:T(8,128)(2,1)S(1)} %copy-done, bf16[128,2048]{1,0:T(8,128)(2,1)S(1)} %copy-done.1, ...), custom_call_target="tpu_custom_call" | custom-call | tf_op jit(solution)/shard_map/norm/pallas_call | solution.py:521
  63.9 6.9 %all-to-all-start.2 = ((f32[64,1,640]{2,1,0:T(1,128)}), f32[64,1,640]{2,1,0:T(1,128)S(1)}, u32[]{:S(2)}, u32[]{:S(2)}) async-start(f32[64,1,640]{2,1,0:T(1,128)} %bitcast.22), calls=%async_computation.2 | async-start | bytes 327680 | tf_op jit(solution)/shard_map/all_to_all | solution.py:557
  70.8 6.2 %back.1 = (bf16[128,2048]{1,0:T(8,128)(2,1)}, bf16[128,2048]{1,0:T(8,128)(2,1)}, f32[2048,128]{1,0:T(8,128)}, f32[64,8,128]{2,1,0:T(8,128)S(1)}) custom-call(f32[2,128,128]{2,1,0:T(8,128)} %get-tuple-element.42.row_hbm, f32[128,2048]{1,0:T(8,128)S(1)} %get-tuple-element.39.mixed_ref, bf16[128,2048]{1,0:T(8,128)(2,1)} %gate_hbm.3, bf16[128,2048]{1,0:T(8,128)(2,1)} %cot_hbm.3, ...), custom_call_target="tpu_custom_call" | custom-call | tf_op jit(solution)/shard_map/back/pallas_call | solution.py:521
  77.0 4.3 %all-to-all-done.2 = f32[64,1,640]{2,1,0:T(1,128)S(1)} async-done(((f32[64,1,640]{2,1,0:T(1,128)}), f32[64,1,640]{2,1,0:T(1,128)S(1)}, u32[]{:S(2)}, u32[]{:S(2)}) %all-to-all-start.2) | async-done | bytes 163872 | tf_op jit(solution)/shard_map/all_to_all | solution.py:557
  81.4 0.5 suffix.1
  81.9 16.4 %all_to_all.21 = f32[64,1,640]{2,1,0:T(1,128)S(1)} all-to-all(f32[64,1,640]{2,1,0:T(1,128)S(1)} %bitcast.13), channel_id=1, replica_groups=mesh['ctx'=64,'tp'=4] {'ctx'}, dimensions={0} | all-to-all | bytes 327680 | tf_op jit(solution)/shard_map/all_to_all | solution.py:557
  98.3 3.5 %grad.1 = (bf16[128,2048]{1,0:T(8,128)(2,1)}, bf16[128,2048]{1,0:T(8,128)(2,1)}, f32[16,128]{1,0:T(8,128)}, f32[16,128]{1,0:T(8,128)}) custom-call(f32[320,128]{1,0:T(8,128)S(1)} %bitcast.11, f32[2048,128]{1,0:T(8,128)} %get-tuple-element.49.local_hbm, bf16[128,2048]{1,0:T(8,128)(2,1)} %k_hbm.3, bf16[128,2048]{1,0:T(8,128)(2,1)} %v_hbm.3, ...), custom_call_target="tpu_custom_call" | custom-call | tf_op jit(solution)/shard_map/grad/pallas_call | solution.py:521
  (3 shorter events, 0.0 us)
Async XLA Ops:
  4.9 13.0 %copy-start.4 = (f32[2048]{0:T(1024)S(1)}, f32[2048]{0:T(1024)}, u32[]{:S(2)}) copy-start(f32[2048]{0:T(1024)} %param.13) | copy-start | bytes 24580
  4.9 13.0 %copy-start.5 = (f32[128,16]{0,1:T(8,128)S(1)}, f32[128,16]{0,1:T(8,128)}, u32[]{:S(2)}) copy-start(f32[128,16]{0,1:T(8,128)} %param.11) | copy-start | bytes 24580
  4.9 25.0 %all-to-all-start = ((f32[64,8,128]{2,1,0:T(8,128)}), f32[64,8,128]{2,1,0:T(8,128)S(1)}, u32[]{:S(2)}, u32[]{:S(2)}) async-start(f32[64,8,128]{2,1,0:T(8,128)} %get-tuple-element.34), calls=%async_computation | async-start | bytes 524288 | tf_op jit(solution)/shard_map/all_to_all | solution.py:557
  30.0 0.7 copy-start.2
  46.9 10.5 %copy-start = (bf16[128,2048]{1,0:T(8,128)(2,1)S(1)}, bf16[128,2048]{1,0:T(8,128)(2,1)}, u32[]{:S(2)}) copy-start(bf16[128,2048]{1,0:T(8,128)(2,1)} %gate_hbm.3) | copy-start | bytes 1572868
  46.9 10.5 %copy-start.1 = (bf16[128,2048]{1,0:T(8,128)(2,1)S(1)}, bf16[128,2048]{1,0:T(8,128)(2,1)}, u32[]{:S(2)}) copy-start(bf16[128,2048]{1,0:T(8,128)(2,1)} %cot_hbm.3) | copy-start | bytes 1572868
  49.4 8.0 %copy-start.3 = (f32[2048]{0:T(1024)S(1)}, f32[2048]{0:T(1024)}, u32[]{:S(2)}) copy-start(f32[2048]{0:T(1024)} %param.14) | copy-start | bytes 24580
  63.9 17.5 %all-to-all-start.2 = ((f32[64,1,640]{2,1,0:T(1,128)}), f32[64,1,640]{2,1,0:T(1,128)S(1)}, u32[]{:S(2)}, u32[]{:S(2)}) async-start(f32[64,1,640]{2,1,0:T(1,128)} %bitcast.22), calls=%async_computation.2 | async-start | bytes 327680 | tf_op jit(solution)/shard_map/all_to_all | solution.py:557
